TPU v7x, 32 devices: a whole 2x2x4 slice. The times are simulated.
32 devices in a mesh: rep: 2 (over core), mp: 16 (over z, y, x).
Axes of the slice: x: 2, y: 2, z: 4, core: 2. Of those that a mesh axis runs over, the one named last changes fastest.
Arguments:
- lookup_block: int32 [2, 2048, 16, 4], P(None, ('rep', 'mp')), may hold values from 0 to 9
- lookup_offset: int32 [2, 2048, 16, 4], P(None, ('rep', 'mp')), may hold values from 0 to 63
- interaction_grad: bfloat16 [2, 2048, 16, 16], P(None, ('rep', 'mp')), may hold values from -4 to 4
- table: bfloat16 [49152, 256], P('mp'), may hold values from -0.3125 to 0.3125
- adagrad_state: float32 [49152], P('mp'), may hold values from 0.05 to 2
- touched_blocks: int32 [16, 10], P('mp'), may hold values from 0 to 47, as said below
- dither: int32 [16, 640, 256], P('mp'), may hold values from 0 to 32767
Outputs:
- new_table: bfloat16 [49152, 256], P('mp')
- new_state: float32 [49152], P('mp')
Inputs may be any that keep to these rules, and one draw needn't show every extreme that they name: `touched_blocks`: each row names 10 different row blocks.
All inputs are finite; a program needn't handle non-finite values.
Results may differ from a plain program's by a relative error of at most 0.00055.
The roundings to bfloat16 on the way count: a program that leaves them out, or rounds other values in their place, can miss the bound.
Values may be sent and summed in bfloat16 or wider, within the bound.
A program may use at most 128 MiB of HBM per device.

v0:
```python
import functools
import math

import jax
import jax.numpy as jnp
from jax import lax
from jax.experimental import pallas as pl
from jax.experimental.pallas import tpu as pltpu
from jax.sharding import PartitionSpec as P

BLOCK = 64
LEARN_RATE = 0.1
POOL_DECAY = 0.5
DITHER_UNIT = 2.0 ** (-15)
SMALLEST = 2.0 ** (-14)
KEEP_BYTES = 8 << 20
MESH = pl.DeviceIdType.MESH


def dither_round(weights, dither_bits):
    magnitude = jnp.maximum(jnp.abs(weights), SMALLEST)
    spacing = jnp.exp2(jnp.floor(jnp.log2(magnitude)) - 7.0)
    grid_level = jnp.floor(weights / spacing + dither_bits.astype(jnp.float32) * DITHER_UNIT)
    return (grid_level * spacing).astype(jnp.bfloat16)


def step_kernel(
    n,
    block_hbm,
    offset_hbm,
    cot_ref,
    touched_ref,
    state_hbm,
    table_ref,
    dither_ref,
    out_ref,
    state_out_ref,
    block_ref,
    offset_ref,
    state_ref,
    rows_ref,
    cot_in,
    near,
    far,
    w_ref,
    w_other,
    table_in,
    dither_in,
    slab,
    slab_t,
    pooled_out,
    pooled_in,
    grad_out,
    grad_in,
    kept,
    total,
    squares,
    rows_new,
    small_sem,
    rows_send,
    near_recv,
    far_recv,
    pooled_send,
    pooled_recv,
    grad_send,
    grad_recv,
):
    me = lax.axis_index("mp")
    rep = lax.axis_index("rep")
    m = n // 2
    group = me // m
    local = lax.rem(me, m)
    mirror = lax.rem(me + m, n)
    samples = w_ref.shape[1]
    bags = rows_ref.shape[3]
    slab_size, width = slab.shape
    touch_count = slab_size // BLOCK
    keeps = kept.shape[1] == m
    columns = pl.ds(pl.multiple_of(rep * width, width), width)

    def at(peer):
        return {"device_id": (rep, peer), "device_id_type": MESH}

    partner = {"device_id": (1 - rep, me), "device_id_type": MESH}

    def each(first, body):
        def run(step, carry):
            body(lax.rem(local + step, m))
            return carry

        lax.fori_loop(first, m, run, 0)

    def near_at(j):
        return group * m + j

    def far_at(j):
        return (1 - group) * m + j

    barrier = pltpu.get_barrier_semaphore()
    each(1, lambda j: pl.semaphore_signal(barrier, inc=1, **at(near_at(j))))
    each(0, lambda j: pl.semaphore_signal(barrier, inc=1, **at(far_at(j))))
    pl.semaphore_signal(barrier, inc=1, **partner)
    block_copy = pltpu.make_async_copy(block_hbm, block_ref, small_sem.at[17])
    block_copy.start()
    offset_copy = pltpu.make_async_copy(offset_hbm, offset_ref, small_sem.at[18])
    offset_copy.start()
    state_copy = pltpu.make_async_copy(state_hbm, state_ref, small_sem.at[19])
    state_copy.start()
    table_copy = pltpu.make_async_copy(table_ref.at[:, :, columns], table_in, small_sem.at[13])
    table_copy.start()
    dither_copy = pltpu.make_async_copy(dither_ref.at[:, columns], dither_in, small_sem.at[14])
    dither_copy.start()
    block_copy.wait()
    offset_copy.wait()
    rows_ref[...] = block_ref[...] * BLOCK + offset_ref[...]
    near[rep, local] = rows_ref[:, :, local]
    total[...] = jnp.zeros_like(total)
    table_copy.wait()
    for block in range(touch_count):
        slab[block * BLOCK : (block + 1) * BLOCK, :] = table_in[touched_ref[0, block]]
    slab_t[0] = slab[...].astype(jnp.float32).T.astype(jnp.bfloat16)
    pl.semaphore_wait(barrier, n)

    def near_copy(j, slot):
        return pltpu.make_async_remote_copy(
            rows_ref.at[:, :, j],
            near.at[rep, slot],
            rows_send.at[0, j],
            near_recv.at[slot],
            **at(near_at(j)),
        )

    def far_copy(j, slot):
        return pltpu.make_async_remote_copy(
            rows_ref.at[:, 1 - group, j],
            far.at[rep, slot],
            rows_send.at[1, j],
            far_recv.at[slot],
            **at(far_at(j)),
        )

    each(1, lambda j: near_copy(j, local).start())
    slab_copy = pltpu.make_async_remote_copy(
        slab_t.at[0], slab_t.at[1], small_sem.at[9], small_sem.at[10], **at(mirror)
    )
    slab_copy.start()
    each(0, lambda j: far_copy(j, local).start())
    cot_size = cot_in.shape[1]

    def spread(chunk, carry):
        cot_copy = pltpu.make_async_copy(
            cot_ref.at[:, pl.ds(chunk * cot_size, cot_size)], cot_in, small_sem.at[0]
        )
        cot_copy.start()
        cot_copy.wait()
        for i in range(cot_size):
            pieces = [cot_in[micro, i].astype(jnp.float32) for micro in range(cot_in.shape[0])]
            at_row = pl.multiple_of((chunk * cot_size + i) * n, n)
            w_ref[pl.ds(at_row, n), :] = jnp.concatenate(pieces, axis=-1)
        return carry

    lax.fori_loop(0, n // cot_size, spread, 0)
    w_copy = pltpu.make_async_remote_copy(
        w_ref, w_other, small_sem.at[1], small_sem.at[2], **partner
    )
    w_copy.start()
    each(1, lambda j: near_copy(j, j).wait_recv())
    swap_near = pltpu.make_async_remote_copy(
        near.at[rep], near.at[rep], small_sem.at[3], small_sem.at[4], **partner
    )
    swap_near.start()

    offset_in_block = lax.broadcasted_iota(jnp.int32, (BLOCK, samples), 0)
    offset_in_block = offset_in_block.astype(jnp.float32).astype(jnp.bfloat16)
    one = jnp.ones((BLOCK, samples), jnp.bfloat16)

    def hits(micros):
        rows = jnp.concatenate([micros[i] for i in range(micros.shape[0])], axis=-1)
        blocks = []
        block_of, offset_of = rows // BLOCK, lax.rem(rows, BLOCK)
        for block in range(slab_size // BLOCK):
            wanted = jnp.where(block_of == block, offset_of, -1).astype(jnp.float32)
            counted = jnp.zeros((BLOCK, samples), jnp.bfloat16)
            for lookup in range(bags):
                row = jnp.broadcast_to(wanted[lookup : lookup + 1, :], (BLOCK, samples))
                same = row.astype(jnp.bfloat16) == offset_in_block
                counted = counted + jnp.where(same, one, jnp.zeros_like(one))
            blocks.append(counted)
        return jnp.concatenate(blocks, axis=0)

    def pooled_copy(part, which, j, slot):
        return pltpu.make_async_remote_copy(
            pooled_out.at[part, which, j],
            pooled_in.at[part, slot],
            pooled_send.at[part, which, j],
            pooled_recv.at[part, slot],
            **at(near_at(j)),
        )

    def grad_copy(part, peer, slot):
        return pltpu.make_async_remote_copy(
            grad_out.at[part, peer],
            grad_in.at[part, slot],
            grad_send.at[part, peer],
            grad_recv.at[part, slot],
            **at(peer),
        )

    def pool(part, replica, which):
        table = group if which == 0 else 1 - group
        feature = me if which == 0 else mirror

        def pooled(j):
            counted = hits(near[replica, j, :, table])
            if which == 0 and keeps:
                kept[part, j] = counted
            return jnp.dot(slab_t[which], counted, preferred_element_type=jnp.float32).astype(
                jnp.bfloat16
            )

        def send(j):
            pooled_out[part, which, j] = pooled(j)
            pooled_copy(part, which, j, feature).start()

        each(1, send)
        pooled_in[part, feature] = pooled(local)

    def interact(part, weights):
        def arrive(j):
            pooled_copy(part, 0, j, near_at(j)).wait_recv()
            pooled_copy(part, 1, j, far_at(j)).wait_recv()

        each(1, arrive)

        def mixed(feature):
            def add(other, carry):
                weight = (
                    weights[pl.ds(feature * n + other, 1), :]
                    + weights[pl.ds(other * n + feature, 1), :]
                )
                return carry + weight * pooled_in[part, other].astype(jnp.float32)

            start = POOL_DECAY * pooled_in[part, feature].astype(jnp.float32)
            return lax.fori_loop(0, n, add, start, unroll=4).astype(jnp.bfloat16)

        def send(peer):
            grad_out[part, peer] = mixed(peer)
            grad_copy(part, peer, me).start()

        each(0, lambda j: send(far_at(j)))
        each(1, lambda j: send(near_at(j)))
        grad_in[part, me] = mixed(me)

    def collect(part, replica):
        def add(peer, counted):
            total[...] += lax.dot_general(
                counted,
                grad_in[part, peer],
                (((1,), (1,)), ((), ())),
                preferred_element_type=jnp.float32,
            )

        def near_hits(j):
            return kept[part, j] if keeps else hits(near[replica, j, :, group])

        def take_near(j):
            grad_copy(part, near_at(j), near_at(j)).wait_recv()
            add(near_at(j), near_hits(j))

        def take_far(j):
            counted = hits(far[replica, j])
            grad_copy(part, far_at(j), far_at(j)).wait_recv()
            add(far_at(j), counted)

        add(me, near_hits(local))
        each(1, take_near)
        each(0, take_far)

    pool(0, rep, 0)
    slab_copy.wait_recv()
    pool(0, rep, 1)
    swap_near.wait_recv()
    pool(1, 1 - rep, 0)
    interact(0, w_ref)
    pool(1, 1 - rep, 1)
    each(0, lambda j: far_copy(j, j).wait_recv())
    swap_far = pltpu.make_async_remote_copy(
        far.at[rep], far.at[rep], small_sem.at[11], small_sem.at[12], **partner
    )
    swap_far.start()
    w_copy.wait_recv()
    interact(1, w_other)
    collect(0, rep)
    swap_far.wait_recv()
    collect(1, 1 - rep)

    state_copy.wait()
    pieces = []
    for block in range(touch_count):
        at_block = touched_ref[0, block]
        pair = state_ref[pl.ds(at_block // 2, 1), :]
        pieces.append(jnp.where(lax.rem(at_block, 2) == 0, pair[:, :BLOCK], pair[:, BLOCK:]))
    state_row = jnp.concatenate(pieces, axis=1)
    grad = total[...]
    squares[0] = jnp.sum((grad * grad).T, axis=0, keepdims=True)
    square_copy = pltpu.make_async_remote_copy(
        squares.at[0], squares.at[1], small_sem.at[5], small_sem.at[6], **partner
    )
    square_copy.start()
    square_copy.wait_recv()
    first = jnp.where(rep == 0, squares[0], squares[1])
    second = jnp.where(rep == 0, squares[1], squares[0])
    state_next = state_row + (first + second) / (2.0 * width)
    divisor = jnp.broadcast_to(jnp.sqrt(state_next) + 1e-08, (width, slab_size)).T
    dither_copy.wait()
    size = slab_size // 2
    new_copies = []
    for piece in range(2):
        part = pl.ds(piece * size, size)
        span = slice(piece * size, (piece + 1) * size)
        moved = slab[span, :].astype(jnp.float32) - LEARN_RATE * total[span, :] / divisor[span]
        rows_new[0, span] = dither_round(moved, dither_in[span, :])
        new_copy = pltpu.make_async_remote_copy(
            rows_new.at[0, part],
            rows_new.at[1, part],
            small_sem.at[7 + 8 * piece],
            small_sem.at[8 + 8 * piece],
            **partner,
        )
        new_copy.start()
        new_copies.append(new_copy)
    out_ref[:, columns] = rows_new[0]
    state_all = state_ref[...]
    block_at = 2 * lax.broadcasted_iota(jnp.int32, state_all.shape, 0)
    block_at = block_at + lax.broadcasted_iota(jnp.int32, state_all.shape, 1) // BLOCK
    for block in range(touch_count):
        piece = state_next[:, block * BLOCK : (block + 1) * BLOCK]
        piece = jnp.broadcast_to(jnp.concatenate([piece, piece], axis=1), state_all.shape)
        state_all = jnp.where(block_at == touched_ref[0, block], piece, state_all)
    state_out_ref[...] = state_all

    each(1, lambda j: near_copy(j, j).wait_send())
    each(0, lambda j: far_copy(j, j).wait_send())
    for part in range(2):
        for which in range(2):
            each(1, lambda j: pooled_copy(part, which, j, j).wait_send())
        each(1, lambda j: grad_copy(part, near_at(j), me).wait_send())
        each(0, lambda j: grad_copy(part, far_at(j), me).wait_send())
    slab_copy.wait_send()
    w_copy.wait_send()
    swap_near.wait_send()
    swap_far.wait_send()
    square_copy.wait_send()
    for new_copy in new_copies:
        new_copy.wait()
    out_ref[:, pl.ds(pl.multiple_of((1 - rep) * width, width), width)] = rows_new[1]


def fused_step(n, blocks, offsets, cot, touched, state, table, dither):
    micros, sample_count = blocks.shape[0], blocks.shape[-1]
    samples = micros * sample_count
    cot_size = math.gcd(n, 16)
    slab_size, emb_width = dither.shape
    width = emb_width // 2
    m = n // 2
    keep = m if 4 * m * slab_size * samples <= KEEP_BYTES else 1
    dma = pltpu.SemaphoreType.DMA
    block = (2, n, width, samples)
    vmem = pl.BlockSpec(memory_space=pltpu.VMEM)
    smem = pl.BlockSpec(memory_space=pltpu.SMEM)
    hbm = pl.BlockSpec(memory_space=pltpu.HBM)
    return pl.pallas_call(
        functools.partial(step_kernel, n),
        out_shape=(
            jax.ShapeDtypeStruct((slab_size, emb_width), jnp.bfloat16),
            jax.ShapeDtypeStruct(state.shape, jnp.float32),
        ),
        in_specs=[hbm, hbm, hbm, smem, hbm, hbm, hbm],
        out_specs=(vmem, vmem),
        scratch_shapes=[
            pltpu.VMEM(blocks.shape, jnp.int32),
            pltpu.VMEM(blocks.shape, jnp.int32),
            pltpu.VMEM(state.shape, jnp.float32),
            pltpu.VMEM(blocks.shape, jnp.int32),
            pltpu.VMEM((micros, cot_size, n, sample_count), jnp.bfloat16),
            pltpu.VMEM((2, m, micros, 2) + blocks.shape[3:], jnp.int32),
            pltpu.VMEM((2, m, micros) + blocks.shape[3:], jnp.int32),
            pltpu.VMEM((n * n, samples), jnp.float32),
            pltpu.VMEM((n * n, samples), jnp.float32),
            pltpu.VMEM(table.shape[:2] + (width,), jnp.bfloat16),
            pltpu.VMEM((slab_size, width), jnp.int32),
            pltpu.VMEM((slab_size, width), jnp.bfloat16),
            pltpu.VMEM((2, width, slab_size), jnp.bfloat16),
            pltpu.VMEM((2, 2, m, width, samples), jnp.bfloat16),
            pltpu.VMEM(block, jnp.bfloat16),
            pltpu.VMEM(block, jnp.bfloat16),
            pltpu.VMEM(block, jnp.bfloat16),
            pltpu.VMEM((2, keep, slab_size, samples), jnp.bfloat16),
            pltpu.VMEM((slab_size, width), jnp.float32),
            pltpu.VMEM((2, 1, slab_size), jnp.float32),
            pltpu.VMEM((2, slab_size, width), jnp.bfloat16),
            dma((20,)),
            dma((2, m)),
            dma((m,)),
            dma((m,)),
            dma((2, 2, m)),
            dma((2, n)),
            dma((2, n)),
            dma((2, n)),
        ],
        compiler_params=pltpu.CompilerParams(collective_id=0, has_side_effects=True),
        name="fused_step",
    )(blocks, offsets, cot, touched, state, table, dither)


def write_kernel(touched_ref, new_ref, state_ref, table_ref, out_ref, state_out_ref, sem):
    state_out_ref[...] = state_ref[...]

    def write(block, carry):
        new = -1
        for i in range(touched_ref.shape[1]):
            new = jnp.where(touched_ref[0, i] == block, i, new)

        @pl.when(new >= 0)
        def _():
            pltpu.make_async_copy(new_ref.at[new], out_ref.at[block], sem).start()

        @pl.when(new < 0)
        def _():
            pltpu.make_async_copy(table_ref.at[block], out_ref.at[block], sem).start()

        return carry

    lax.fori_loop(0, table_ref.shape[0], write, 0)
    pltpu.make_async_copy(table_ref, out_ref, sem).wait()


def write_table(touched, new_rows, state, table):
    vmem = pl.BlockSpec(memory_space=pltpu.VMEM)
    return pl.pallas_call(
        write_kernel,
        out_shape=(
            jax.ShapeDtypeStruct(table.shape, table.dtype),
            jax.ShapeDtypeStruct(state.shape, state.dtype),
        ),
        in_specs=[pl.BlockSpec(memory_space=pltpu.SMEM), vmem, vmem, vmem],
        out_specs=(pl.BlockSpec(memory_space=pl.ANY), vmem),
        scratch_shapes=[pltpu.SemaphoreType.DMA],
        name="write_table",
    )(touched, new_rows, state, table)


def per_device(
    lookup_block, lookup_offset, interaction_grad, table, adagrad_state, touched_blocks, dither
):
    micro_count, sample_count, feature_count, bag_count = lookup_block.shape
    n = lax.axis_size("mp")
    row_count, emb_width = table.shape
    touch_count = touched_blocks.shape[1]
    split = (micro_count, 2, feature_count // 2, bag_count, sample_count)
    blocks = lookup_block.transpose(0, 2, 3, 1).reshape(split)
    offsets = lookup_offset.transpose(0, 2, 3, 1).reshape(split)
    cot = interaction_grad.transpose(0, 2, 3, 1)
    table_blocks = table.reshape(row_count // BLOCK, BLOCK, emb_width)
    state = adagrad_state.reshape(row_count // (2 * BLOCK), 2 * BLOCK)
    new_rows, new_state = fused_step(
        n, blocks, offsets, cot, touched_blocks, state, table_blocks, dither[0]
    )
    new_rows = new_rows.reshape(touch_count, BLOCK, emb_width)
    new_table, new_state = write_table(touched_blocks, new_rows, new_state, table_blocks)
    return (new_table.reshape(row_count, emb_width), new_state.reshape(row_count))


def solution(mesh):
    return jax.shard_map(
        per_device,
        mesh=mesh,
        in_specs=(
            P(None, ("rep", "mp"), None, None),
            P(None, ("rep", "mp"), None, None),
            P(None, ("rep", "mp"), None, None),
            P("mp", None),
            P("mp"),
            P("mp", None),
            P("mp", None, None),
        ),
        out_specs=(P("mp", None), P("mp")),
        check_vma=False,
    )
```

profile of v0, /device:TPU:0, one launch (start us, length us, event | category | flops | bytes accessed | tf_op | source)
XLA Modules:
  0.0 59.4 jit_solution(5475789017468357700)
XLA Ops:
  0.6 55.3 %fused_step.1 = (bf16[640,256]{1,0:T(8,128)(2,1)}, f32[24,128]{1,0:T(8,128)}) custom-call(s32[2,2,8,4,64]{4,3,2,1,0:T(4,128)} %bitcast.18, s32[2,2,8,4,64]{4,3,2,1,0:T(4,128)} %bitcast.19, bf16[2,16,16,64]{3,2,1,0:T(8,128)(2,1)} %bitcast.17, s32[1,10]{1,0:T(1,128)} %touched_ref.3, f32[24,128]{1,0:T(8,128)} %bitcast.20, bf16[48,64,256]{2,1,0:T(8,128)(2,1)} %bitcast.13, ...), custom_call_target="tpu_custom_call" | custom-call | tf_op jit(solution)/shard_map/fused_step/pallas_call | solution.py:372
  55.9 3.5 %write_table.1 = (bf16[48,64,256]{2,1,0:T(8,128)(2,1)}, f32[24,128]{1,0:T(8,128)}) custom-call(s32[1,10]{1,0:T(1,128)} %touched_ref.3, bf16[10,64,256]{2,1,0:T(8,128)(2,1)} %bitcast.16, f32[24,128]{1,0:T(8,128)} %get-tuple-element.7.state_ref, bf16[48,64,256]{2,1,0:T(8,128)(2,1)} %bitcast.14), custom_call_target="tpu_custom_call" | custom-call | tf_op jit(solution)/shard_map/write_table/pallas_call | solution.py:440
where the time goes:
time: 59.6 us; the launch traced here: 59.4 us
  Pallas kernels  58.8 us (99%)
  between operations  0.64 us (1%)
    pallas_call x1, Pallas kernels, fused_step(): pl.pallas_call(functools.partial(step_kernel, n), out_shape=(jax.ShapeDty...  55.3 us
    pallas_call x1, Pallas kernels, write_table(): pl.pallas_call(write_kernel, out_shape=(jax.ShapeDtypeStruct(table.shape,...  3.47 us

commit v1 on v0

v1 whole, which is shorter than its diff:
```python
import functools
import math

import jax
import jax.numpy as jnp
from jax import lax
from jax.experimental import pallas as pl
from jax.experimental.pallas import tpu as pltpu
from jax.sharding import PartitionSpec as P

BLOCK = 64
PLANES = 4
PARTS = 2
LEARN_RATE = 0.1
POOL_DECAY = 0.5
DITHER_UNIT = 2.0 ** (-15)
SMALLEST = 2.0 ** (-14)
KEEP_BYTES = 8 << 20
MESH = pl.DeviceIdType.MESH


def dither_round(weights, dither_bits):
    magnitude = jnp.maximum(jnp.abs(weights), SMALLEST)
    spacing = jnp.exp2(jnp.floor(jnp.log2(magnitude)) - 7.0)
    grid_level = jnp.floor(weights / spacing + dither_bits.astype(jnp.float32) * DITHER_UNIT)
    return (grid_level * spacing).astype(jnp.bfloat16)


def plane_order(planes, plane, step):
    picked = jnp.int32(0)
    for own in range(planes):
        near_first = sorted(range(planes), key=lambda q: (abs(q - own), (q - own) * (2 * own - planes)))
        picked = jnp.where(plane == own, near_first[step], picked)
    return picked


def step_kernel(
    n,
    block_hbm,
    offset_hbm,
    cot_ref,
    touched_ref,
    state_hbm,
    table_ref,
    dither_ref,
    out_ref,
    state_out_ref,
    table_in,
    block_ref,
    offset_ref,
    state_ref,
    rows_ref,
    cot_in,
    near,
    far,
    w_ref,
    dither_in,
    slab,
    slabs,
    pooled_out,
    pooled_in,
    grad_out,
    grad_in,
    kept,
    kept_own,
    total,
    total_in,
    state_col,
    local_sem,
    pair_sem,
    near_send,
    near_recv,
    far_send,
    far_recv,
    slab_send,
    slab_recv,
    half_send,
    half_recv,
    pooled_send,
    pooled_recv,
    grad_send,
    grad_recv,
):
    me = lax.axis_index("mp")
    rep = lax.axis_index("rep")
    planes, parts = slabs.shape[0], slabs.shape[1]
    m = n // planes
    plane = me // m
    local = lax.rem(me, m)
    samples = w_ref.shape[1]
    bags = rows_ref.shape[3]
    slab_size, width = slab.shape
    columns = width // parts
    touch_count = slab_size // BLOCK
    keeps = kept.shape[0] == planes

    def at(peer):
        return {"device_id": (rep, peer), "device_id_type": MESH}

    partner = {"device_id": (1 - rep, me), "device_id_type": MESH}

    def each(first, body):
        def run(step, carry):
            body(lax.rem(local + step, m))
            return carry

        lax.fori_loop(first, m, run, 0)

    def others(body):
        def run(step, carry):
            body(lax.rem(me + step, n))
            return carry

        lax.fori_loop(1, n, run, 0)

    def outside(body, first=0, last=n - m):
        def run(step, carry):
            body(lax.rem(plane + 1 + step // m, planes), lax.rem(local + step, m))
            return carry

        lax.fori_loop(first, last, run, 0)

    def nearest(step):
        return plane_order(planes, plane, step)

    barrier = pltpu.get_barrier_semaphore()
    others(lambda peer: pl.semaphore_signal(barrier, inc=1, **at(peer)))
    pl.semaphore_signal(barrier, inc=1, **partner)
    table_copy = pltpu.make_async_copy(table_ref, table_in, local_sem.at[0])
    table_copy.start()
    block_copy = pltpu.make_async_copy(block_hbm, block_ref, local_sem.at[1])
    block_copy.start()
    offset_copy = pltpu.make_async_copy(offset_hbm, offset_ref, local_sem.at[2])
    offset_copy.start()
    state_copy = pltpu.make_async_copy(state_hbm, state_ref, local_sem.at[3])
    state_copy.start()
    dither_copy = pltpu.make_async_copy(dither_ref, dither_in, local_sem.at[4])
    dither_copy.start()
    block_copy.wait()
    offset_copy.wait()
    rows_ref[...] = block_ref[...] * BLOCK + offset_ref[...]
    near[local] = rows_ref[:, :, local]
    table_copy.wait()
    for block in range(touch_count):
        slab[block * BLOCK : (block + 1) * BLOCK, :] = table_in[touched_ref[0, block]]
    for part in range(parts):
        turned = slab[:, part * columns : (part + 1) * columns].astype(jnp.float32).T
        slabs[plane, part] = turned.astype(jnp.bfloat16).reshape(slabs.shape[2:])
    pl.semaphore_wait(barrier, n)

    def near_copy(j, slot):
        return pltpu.make_async_remote_copy(
            rows_ref.at[:, :, j],
            near.at[slot],
            near_send.at[j],
            near_recv.at[slot],
            **at(plane * m + j),
        )

    def far_copy(q, j, slot):
        return pltpu.make_async_remote_copy(
            rows_ref.at[:, q, j],
            far.at[slot],
            far_send.at[q * m + j],
            far_recv.at[slot],
            **at(q * m + j),
        )

    def slab_copy(part, q, way, peer):
        return pltpu.make_async_remote_copy(
            slabs.at[q, part, rep],
            slabs.at[q, part, rep],
            slab_send.at[way, part, q],
            slab_recv.at[part, q],
            **at(peer),
        )

    def half_copy(part, q, which):
        return pltpu.make_async_remote_copy(
            slabs.at[q, part, which],
            slabs.at[q, part, which],
            half_send.at[part, q],
            half_recv.at[part, q],
            **partner,
        )

    has_up, has_down = plane + 1 < planes, plane > 0
    inner = jnp.logical_and(has_up, has_down)
    outer = jnp.logical_not(inner)
    up, down = lax.rem(me + m, n), lax.rem(me + n - m, n)

    def own_slab(part, act):
        @pl.when(has_up)
        def _():
            act(slab_copy(part, plane, 0, up))

        @pl.when(has_down)
        def _():
            act(slab_copy(part, plane, 1, down))

    def passed_slab(part, q, act):
        @pl.when(jnp.logical_and(q < plane, has_up))
        def _():
            act(slab_copy(part, q, 0, up))

        @pl.when(jnp.logical_and(q > plane, has_down))
        def _():
            act(slab_copy(part, q, 1, down))

    each(1, lambda j: near_copy(j, local).start())
    own_slab(0, lambda copy: copy.start())
    outside(lambda q, j: far_copy(q, j, me).start())
    for part in range(1, parts):
        own_slab(part, lambda copy: copy.start())
    cot_size = cot_in.shape[1]

    def spread(chunk, carry):
        cot_copy = pltpu.make_async_copy(
            cot_ref.at[:, pl.ds(chunk * cot_size, cot_size)], cot_in, local_sem.at[5]
        )
        cot_copy.start()
        cot_copy.wait()
        for i in range(cot_size):
            pieces = [cot_in[micro, i].astype(jnp.float32) for micro in range(cot_in.shape[0])]
            at_row = pl.multiple_of((chunk * cot_size + i) * n, n)
            w_ref[pl.ds(at_row, n), :] = jnp.concatenate(pieces, axis=-1)
        return carry

    lax.fori_loop(0, n // cot_size, spread, 0)
    place = lax.broadcasted_iota(jnp.int32, (n, samples), 0)

    def fold(f, carry):
        along = pl.ds(pl.multiple_of(f * n, n), n)
        across = pl.ds(f, n, stride=n)
        row, column = w_ref[along, :], w_ref[across, :]
        both = row + column + jnp.where(place == f, POOL_DECAY, 0.0)
        w_ref[along, :] = jnp.where(place >= f, both, row)
        w_ref[across, :] = jnp.where(place >= f, both, column)
        return carry

    lax.fori_loop(0, n, fold, 0)
    total[...] = jnp.zeros_like(total)

    offset_in_block = lax.broadcasted_iota(jnp.int32, (BLOCK, samples), 0)
    offset_in_block = offset_in_block.astype(jnp.float32).astype(jnp.bfloat16)
    one = jnp.ones((BLOCK, samples), jnp.bfloat16)

    def hits(micros):
        rows = jnp.concatenate([micros[i] for i in range(micros.shape[0])], axis=-1)
        blocks = []
        block_of, offset_of = rows // BLOCK, lax.rem(rows, BLOCK)
        for block in range(slab_size // BLOCK):
            wanted = jnp.where(block_of == block, offset_of, -1).astype(jnp.float32)
            counted = jnp.zeros((BLOCK, samples), jnp.bfloat16)
            for lookup in range(bags):
                row = jnp.broadcast_to(wanted[lookup : lookup + 1, :], (BLOCK, samples))
                same = row.astype(jnp.bfloat16) == offset_in_block
                counted = counted + jnp.where(same, one, jnp.zeros_like(one))
            blocks.append(counted)
        return jnp.concatenate(blocks, axis=0)

    def pooled_copy(part, q, j, slot):
        return pltpu.make_async_remote_copy(
            pooled_out.at[part, q, j],
            pooled_in.at[part, q * m + slot],
            pooled_send.at[part, q, j],
            pooled_recv.at[part, q * m + slot],
            **at(plane * m + j),
        )

    def grad_copy(part, peer, slot):
        return pltpu.make_async_remote_copy(
            grad_out.at[part, peer],
            grad_in.at[part, slot],
            grad_send.at[part, peer],
            grad_recv.at[part, slot],
            **at(peer),
        )

    def pool(part, q):
        rows_of = slabs[q, part].reshape(columns, slab_size)

        def pooled(j):
            if keeps and part > 0:
                counted = kept[q, j]
            else:
                counted = hits(near[j, :, q])
                if keeps:
                    kept[q, j] = counted
            summed = jnp.dot(rows_of, counted, preferred_element_type=jnp.float32)
            return summed.astype(jnp.bfloat16)

        def send(j):
            pooled_out[part, q, j] = pooled(j)
            pooled_copy(part, q, j, local).start()

        each(1, send)
        pooled_in[part, q * m + local] = pooled(local)

    def relay(part, step):
        q = nearest(step)
        slab_copy(part, q, 0, up).wait_recv()
        passed_slab(part, q, lambda copy: copy.start())
        half_copy(part, q, rep).start()

    def pool_from(part, step):
        q = nearest(step)
        half_copy(part, q, 1 - rep).wait_recv()
        pool(part, q)

    def arrive(part):
        def take(j):
            for q in range(planes):
                pooled_copy(part, q, j, j).wait_recv()

        each(1, take)

    def interact(part):
        def mixed(feature):
            def add(other, carry):
                weight = w_ref[pl.ds(feature * n + other, 1), :]
                return carry + weight * pooled_in[part, other].astype(jnp.float32)

            start = jnp.zeros((columns, samples), jnp.float32)
            return lax.fori_loop(0, n, add, start, unroll=4).astype(jnp.bfloat16)

        def send(peer):
            grad_out[part, peer] = mixed(peer)
            grad_copy(part, peer, me).start()

        for step in range(planes - 1, 0, -1):
            q = nearest(step)
            each(0, lambda j: send(q * m + j))
        each(1, lambda j: send(plane * m + j))
        grad_in[part, me] = mixed(me)

    def keep_far(first, last):
        def take(q, j):
            peer = q * m + j
            far_copy(q, j, peer).wait_recv()
            if keeps:
                kept_own[peer] = hits(far[peer])

        outside(take, first, last)

    def collect(part):
        def add(peer, counted):
            total[part] += lax.dot_general(
                counted,
                grad_in[part, peer],
                (((1,), (1,)), ((), ())),
                preferred_element_type=jnp.float32,
            )

        def near_hits(j):
            return kept[plane, j] if keeps else hits(near[j, :, plane])

        def take_near(j):
            grad_copy(part, plane * m + j, plane * m + j).wait_recv()
            add(plane * m + j, near_hits(j))

        def take_far(q, j):
            peer = q * m + j
            grad_copy(part, peer, peer).wait_recv()
            add(peer, kept_own[peer] if keeps else hits(far[peer]))

        add(me, near_hits(local))
        each(1, take_near)
        for step in range(1, planes):
            q = nearest(step)
            each(0, lambda j: take_far(q, j))

    each(1, lambda j: near_copy(j, j).wait_recv())
    pool(0, plane)
    relay(0, 1)
    pl.when(inner)(lambda: relay(0, 2))
    pool_from(0, 1)
    relay(1, 1)
    pl.when(inner)(lambda: relay(1, 2))
    pool(1, plane)
    pl.when(inner)(lambda: relay(0, 3))
    pool_from(1, 1)
    pl.when(outer)(lambda: relay(0, 2))
    pool_from(0, 2)
    pl.when(inner)(lambda: relay(1, 3))
    pl.when(outer)(lambda: relay(1, 2))
    pool_from(1, 2)
    pl.when(outer)(lambda: relay(0, 3))
    pool_from(0, 3)
    pl.when(outer)(lambda: relay(1, 3))
    pool_from(1, 3)
    early = jnp.where(inner, 0, n - m)
    keep_far(0, early)
    arrive(0)
    pl.when(outer)(lambda: arrive(1))
    interact(0)
    keep_far(early, n - m)
    pl.when(inner)(lambda: arrive(1))
    interact(1)
    state_copy.wait()
    pieces = []
    for block in range(touch_count):
        at_block = touched_ref[0, block]
        pair = state_ref[pl.ds(at_block // 2, 1), :]
        pieces.append(jnp.where(lax.rem(at_block, 2) == 0, pair[:, :BLOCK], pair[:, BLOCK:]))
    state_row = jnp.concatenate(pieces, axis=1)
    state_col[...] = jnp.broadcast_to(state_row, (state_col.shape[1], slab_size)).T
    def total_copy(part):
        return pltpu.make_async_remote_copy(
            total.at[part], total_in.at[part], pair_sem.at[0, part], pair_sem.at[1, part], **partner
        )

    collect(0)
    total_copy(0).start()
    each(1, lambda j: near_copy(j, j).wait_send())
    outside(lambda q, j: far_copy(q, j, me).wait_send())
    for part in range(parts):
        own_slab(part, lambda copy: copy.wait_send())
        for step in range(1, planes):
            q = nearest(step)
            passed_slab(part, q, lambda copy: copy.wait_send())
            half_copy(part, q, rep).wait_send()
        for q in range(planes):
            each(1, lambda j: pooled_copy(part, q, j, j).wait_send())
    others(lambda peer: grad_copy(0, peer, me).wait_send())
    dither_copy.wait()
    collect(1)
    total_copy(1).start()
    others(lambda peer: grad_copy(1, peer, me).wait_send())
    for part in range(parts):
        total_copy(part).wait_recv()

    def update(block, carry):
        at_rows = pl.ds(pl.multiple_of(block * BLOCK, BLOCK), BLOCK)
        grad = [total[part, at_rows, :] + total_in[part, at_rows, :] for part in range(parts)]
        grad = jnp.concatenate(grad, axis=1)
        state_next = state_col[at_rows, :] + jnp.sum(grad * grad, axis=1, keepdims=True) / width
        state_col[at_rows, :] = state_next
        divisor = jnp.sqrt(state_next) + 1e-08
        divisor = jnp.concatenate([divisor] * (width // divisor.shape[1]), axis=1)
        moved = slab[at_rows, :].astype(jnp.float32) - LEARN_RATE * grad / divisor
        out_ref[at_rows, :] = dither_round(moved, dither_in[at_rows, :])
        return carry

    lax.fori_loop(0, touch_count, update, 0, unroll=2)
    state_all = state_ref[...]
    block_at = 2 * lax.broadcasted_iota(jnp.int32, state_all.shape, 0)
    block_at = block_at + lax.broadcasted_iota(jnp.int32, state_all.shape, 1) // BLOCK
    state_row = state_col[...].T[:1, :]
    for block in range(touch_count):
        piece = state_row[:, block * BLOCK : (block + 1) * BLOCK]
        piece = jnp.broadcast_to(jnp.concatenate([piece, piece], axis=1), state_all.shape)
        state_all = jnp.where(block_at == touched_ref[0, block], piece, state_all)
    state_out_ref[...] = state_all
    for part in range(parts):
        total_copy(part).wait_send()


def fused_step(n, blocks, offsets, cot, touched, state, table, dither):
    micros, planes, m = blocks.shape[0], blocks.shape[1], blocks.shape[2]
    sample_count = blocks.shape[-1]
    samples = micros * sample_count
    cot_size = math.gcd(n, 16)
    slab_size, width = dither.shape
    columns = width // PARTS
    keeps = 2 * n * slab_size * samples <= KEEP_BYTES
    dma = pltpu.SemaphoreType.DMA
    block = (PARTS, n, columns, samples)
    vmem = pl.BlockSpec(memory_space=pltpu.VMEM)
    smem = pl.BlockSpec(memory_space=pltpu.SMEM)
    hbm = pl.BlockSpec(memory_space=pltpu.HBM)
    return pl.pallas_call(
        functools.partial(step_kernel, n),
        out_shape=(
            pltpu.VMEM((slab_size, width), jnp.bfloat16),
            pltpu.VMEM(state.shape, jnp.float32),
            pltpu.VMEM(table.shape, jnp.bfloat16),
        ),
        in_specs=[hbm, hbm, hbm, smem, hbm, hbm, hbm],
        out_specs=(vmem, vmem, vmem),
        scratch_shapes=[
            pltpu.VMEM(blocks.shape, jnp.int32),
            pltpu.VMEM(blocks.shape, jnp.int32),
            pltpu.VMEM(state.shape, jnp.float32),
            pltpu.VMEM(blocks.shape, jnp.int32),
            pltpu.VMEM((micros, cot_size, n, sample_count), jnp.bfloat16),
            pltpu.VMEM((m, micros, planes) + blocks.shape[3:], jnp.int32),
            pltpu.VMEM((n, micros) + blocks.shape[3:], jnp.int32),
            pltpu.VMEM((n * n, samples), jnp.float32),
            pltpu.VMEM((slab_size, width), jnp.int32),
            pltpu.VMEM((slab_size, width), jnp.bfloat16),
            pltpu.VMEM((planes, PARTS, 2, columns // 2, slab_size), jnp.bfloat16),
            pltpu.VMEM((PARTS, planes, m, columns, samples), jnp.bfloat16),
            pltpu.VMEM(block, jnp.bfloat16),
            pltpu.VMEM(block, jnp.bfloat16),
            pltpu.VMEM(block, jnp.bfloat16),
            pltpu.VMEM((planes if keeps else 1, m if keeps else 1, slab_size, samples), jnp.bfloat16),
            pltpu.VMEM((n if keeps else 1, slab_size, samples), jnp.bfloat16),
            pltpu.VMEM((PARTS, slab_size, columns), jnp.float32),
            pltpu.VMEM((PARTS, slab_size, columns), jnp.float32),
            pltpu.VMEM((slab_size, 128), jnp.float32),
            dma((6,)),
            dma((2, PARTS)),
            dma((m,)),
            dma((m,)),
            dma((n,)),
            dma((n,)),
            dma((2, PARTS, planes)),
            dma((PARTS, planes)),
            dma((PARTS, planes)),
            dma((PARTS, planes)),
            dma((PARTS, planes, m)),
            dma((PARTS, n)),
            dma((PARTS, n)),
            dma((PARTS, n)),
        ],
        compiler_params=pltpu.CompilerParams(collective_id=0, has_side_effects=True),
        name="fused_step",
    )(blocks, offsets, cot, touched, state, table, dither)


def write_kernel(touched_ref, new_ref, state_ref, table_ref, out_ref, state_out_ref, place, sem):
    state_copy = pltpu.make_async_copy(state_ref, state_out_ref, sem.at[1])
    state_copy.start()
    blocks, touch_count = table_ref.shape[0], touched_ref.shape[1]

    def clear(block, carry):
        place[block] = -1
        return carry

    lax.fori_loop(0, blocks, clear, 0, unroll=8)
    for i in range(touch_count):
        place[touched_ref[0, i]] = i

    def write(block, carry):
        new = place[block]

        @pl.when(new >= 0)
        def _():
            pltpu.make_async_copy(new_ref.at[new], out_ref.at[block], sem.at[0]).start()

        @pl.when(new < 0)
        def _():
            pltpu.make_async_copy(table_ref.at[block], out_ref.at[block], sem.at[0]).start()

        return carry

    lax.fori_loop(0, blocks, write, 0)
    pltpu.make_async_copy(table_ref, out_ref, sem.at[0]).wait()
    state_copy.wait()


def write_table(touched, new_rows, state, table):
    vmem = pl.BlockSpec(memory_space=pltpu.VMEM)
    hbm = pl.BlockSpec(memory_space=pltpu.HBM)
    held = [pltpu.with_memory_space_constraint(x, pltpu.VMEM) for x in (new_rows, state, table)]
    return pl.pallas_call(
        write_kernel,
        out_shape=(
            jax.ShapeDtypeStruct(table.shape, table.dtype),
            jax.ShapeDtypeStruct(state.shape, state.dtype),
        ),
        in_specs=[pl.BlockSpec(memory_space=pltpu.SMEM), vmem, vmem, vmem],
        out_specs=(hbm, hbm),
        scratch_shapes=[pltpu.SMEM((table.shape[0],), jnp.int32), pltpu.SemaphoreType.DMA((2,))],
        compiler_params=pltpu.CompilerParams(vmem_limit_bytes=4 << 20),
        name="write_table",
    )(touched, *held)


def per_device(
    lookup_block, lookup_offset, interaction_grad, table, adagrad_state, touched_blocks, dither
):
    micro_count, sample_count, feature_count, bag_count = lookup_block.shape
    n = lax.axis_size("mp")
    row_count, emb_width = table.shape
    touch_count = touched_blocks.shape[1]
    split = (micro_count, PLANES, feature_count // PLANES, bag_count, sample_count)
    blocks = lookup_block.transpose(0, 2, 3, 1).reshape(split)
    offsets = lookup_offset.transpose(0, 2, 3, 1).reshape(split)
    cot = interaction_grad.transpose(0, 2, 3, 1)
    table_blocks = table.reshape(row_count // BLOCK, BLOCK, emb_width)
    state = adagrad_state.reshape(row_count // (2 * BLOCK), 2 * BLOCK)
    new_rows, new_state, table_copy = fused_step(
        n, blocks, offsets, cot, touched_blocks, state, table_blocks, dither[0]
    )
    new_rows = new_rows.reshape(touch_count, BLOCK, emb_width)
    new_table, new_state = write_table(touched_blocks, new_rows, new_state, table_copy)
    return (new_table.reshape(row_count, emb_width), new_state.reshape(row_count))


def solution(mesh):
    return jax.shard_map(
        per_device,
        mesh=mesh,
        in_specs=(
            P(None, ("rep", "mp"), None, None),
            P(None, ("rep", "mp"), None, None),
            P(None, ("rep", "mp"), None, None),
            P("mp", None),
            P("mp"),
            P("mp", None),
            P("mp", None, None),
        ),
        out_specs=(P("mp", None), P("mp")),
        check_vma=False,
    )
```

time: 59.6 us -> 56.6 us (0.950)
  the two profiles are of different devices: /device:TPU:0 before, /device:TPU:11 now
where the time goes in v1:
time: 56.6 us; the launch traced here: 56.4 us
  Pallas kernels  55.8 us (99%)
  between operations  0.66 us (1%)
    pallas_call x1, Pallas kernels, fused_step(): pl.pallas_call(functools.partial(step_kernel, n), out_shape=(pltpu.VMEM((...  54 us
    pallas_call x1, Pallas kernels, write_table(): pl.pallas_call(write_kernel, out_shape=(jax.ShapeDtypeStruct(table.shape,...  1.74 us

profile of v1, /device:TPU:11, one launch (start us, length us, event | category | flops | bytes accessed | tf_op | source)
XLA Modules:
  0.0 56.4 jit_solution(5842179724970945158)
XLA Ops:
  0.6 0.0 copy-start
  0.6 54.0 %fused_step.1 = (bf16[640,256]{1,0:T(8,128)(2,1)S(1)}, f32[24,128]{1,0:T(8,128)S(1)}, bf16[48,64,256]{2,1,0:T(8,128)(2,1)S(1)}) custom-call(s32[2,4,4,4,64]{4,3,2,1,0:T(4,128)} %bitcast.17, s32[2,4,4,4,64]{4,3,2,1,0:T(4,128)} %bitcast.18, bf16[2,16,16,64]{3,2,1,0:T(8,128)(2,1)} %bitcast.16, s32[1,10]{1,0:T(1,128)} %touched_ref.3, f32[24,128]{1,0:T(8,128)} %bitcast.19, ...), custom_call_target="tpu_custom_call" | custom-call | tf_op jit(solution)/shard_map/fused_step/pallas_call | solution.py:472
  54.7 0.0 copy-done
  54.7 1.7 %write_table.1 = (bf16[48,64,256]{2,1,0:T(8,128)(2,1)}, f32[24,128]{1,0:T(8,128)}) custom-call(s32[1,10]{1,0:T(1,128)S(1)} %copy-done, bf16[10,64,256]{2,1,0:T(8,128)(2,1)S(1)} %bitcast.13, f32[24,128]{1,0:T(8,128)S(1)} %get-tuple-element.8.state_ref, bf16[48,64,256]{2,1,0:T(8,128)(2,1)S(1)} %get-tuple-element.9.table_ref), custom_call_target="tpu_custom_call" | custom-call | tf_op jit(solution)/shard_map/write_table/pallas_call | solution.py:557
Async XLA Ops:
  0.6 54.0 %copy-start = (s32[1,10]{1,0:T(1,128)S(1)}, s32[1,10]{1,0:T(1,128)}, u32[]{:S(2)}) copy-start(s32[1,10]{1,0:T(1,128)} %touched_ref.3) | copy-start | bytes 124

commit v2 on v1

--- a/solution.py
+++ b/solution.py
@@ -152,8 +152,8 @@
         return pltpu.make_async_remote_copy(
             rows_ref.at[:, :, j],
             near.at[slot],
-            near_send.at[j],
-            near_recv.at[slot],
+            near_send,
+            near_recv,
             **at(plane * m + j),
         )
 
@@ -161,8 +161,8 @@
         return pltpu.make_async_remote_copy(
             rows_ref.at[:, q, j],
             far.at[slot],
-            far_send.at[q * m + j],
-            far_recv.at[slot],
+            far_send,
+            far_recv,
             **at(q * m + j),
         )
 
@@ -179,7 +179,7 @@
         return pltpu.make_async_remote_copy(
             slabs.at[q, part, which],
             slabs.at[q, part, which],
-            half_send.at[part, q],
+            half_send,
             half_recv.at[part, q],
             **partner,
         )
@@ -210,8 +210,11 @@
     each(1, lambda j: near_copy(j, local).start())
     own_slab(0, lambda copy: copy.start())
     outside(lambda q, j: far_copy(q, j, me).start())
-    for part in range(1, parts):
-        own_slab(part, lambda copy: copy.start())
+
+    @pl.when(outer)
+    def _():
+        own_slab(1, lambda copy: copy.start())
+
     cot_size = cot_in.shape[1]
 
     def spread(chunk, carry):
@@ -263,8 +266,8 @@
         return pltpu.make_async_remote_copy(
             pooled_out.at[part, q, j],
             pooled_in.at[part, q * m + slot],
-            pooled_send.at[part, q, j],
-            pooled_recv.at[part, q * m + slot],
+            pooled_send.at[part],
+            pooled_recv.at[part],
             **at(plane * m + j),
         )
 
@@ -272,7 +275,7 @@
         return pltpu.make_async_remote_copy(
             grad_out.at[part, peer],
             grad_in.at[part, slot],
-            grad_send.at[part, peer],
+            grad_send.at[part],
             grad_recv.at[part, slot],
             **at(peer),
         )
@@ -308,12 +311,12 @@
         half_copy(part, q, 1 - rep).wait_recv()
         pool(part, q)
 
+    def batch(ref, send_sem, recv_sem):
+        return pltpu.make_async_remote_copy(ref, ref, send_sem, recv_sem, **partner)
+
     def arrive(part):
-        def take(j):
-            for q in range(planes):
-                pooled_copy(part, q, j, j).wait_recv()
-
-        each(1, take)
+        arrived = pooled_in.at[part, pl.ds(0, planes * (m - 1))]
+        batch(arrived, pooled_send.at[part], pooled_recv.at[part]).wait_recv()
 
     def interact(part):
         def mixed(feature):
@@ -337,11 +340,10 @@
     def keep_far(first, last):
         def take(q, j):
             peer = q * m + j
-            far_copy(q, j, peer).wait_recv()
-            if keeps:
-                kept_own[peer] = hits(far[peer])
-
-        outside(take, first, last)
+            kept_own[peer] = hits(far[peer])
+
+        if keeps:
+            outside(take, first, last)
 
     def collect(part):
         def add(peer, counted):
@@ -370,33 +372,47 @@
             q = nearest(step)
             each(0, lambda j: take_far(q, j))
 
-    each(1, lambda j: near_copy(j, j).wait_recv())
+    batch(near.at[pl.ds(0, m - 1)], near_send, near_recv).wait_recv()
     pool(0, plane)
     relay(0, 1)
-    pl.when(inner)(lambda: relay(0, 2))
-    pool_from(0, 1)
-    relay(1, 1)
-    pl.when(inner)(lambda: relay(1, 2))
-    pool(1, plane)
-    pl.when(inner)(lambda: relay(0, 3))
-    pool_from(1, 1)
-    pl.when(outer)(lambda: relay(0, 2))
-    pool_from(0, 2)
-    pl.when(inner)(lambda: relay(1, 3))
-    pl.when(outer)(lambda: relay(1, 2))
-    pool_from(1, 2)
-    pl.when(outer)(lambda: relay(0, 3))
-    pool_from(0, 3)
-    pl.when(outer)(lambda: relay(1, 3))
-    pool_from(1, 3)
-    early = jnp.where(inner, 0, n - m)
-    keep_far(0, early)
+
+    @pl.when(inner)
+    def _():
+        relay(0, 2)
+        own_slab(1, lambda copy: copy.start())
+        pool(1, plane)
+        pool_from(0, 1)
+        pool_from(0, 2)
+        relay(0, 3)
+        relay(1, 1)
+        relay(1, 2)
+        pool_from(0, 3)
+        pool_from(1, 1)
+        pool_from(1, 2)
+        relay(1, 3)
+        pool_from(1, 3)
+
+    @pl.when(outer)
+    def _():
+        pool(1, plane)
+        pool_from(0, 1)
+        relay(1, 1)
+        relay(0, 2)
+        pool_from(1, 1)
+        pool_from(0, 2)
+        relay(1, 2)
+        relay(0, 3)
+        pool_from(1, 2)
+        pool_from(0, 3)
+        relay(1, 3)
+        pool_from(1, 3)
+
     arrive(0)
-    pl.when(outer)(lambda: arrive(1))
     interact(0)
-    keep_far(early, n - m)
-    pl.when(inner)(lambda: arrive(1))
+    arrive(1)
     interact(1)
+    batch(far.at[pl.ds(0, n - m)], far_send, far_recv).wait_recv()
+    keep_far(0, n - m)
     state_copy.wait()
     pieces = []
     for block in range(touch_count):
@@ -412,21 +428,25 @@
 
     collect(0)
     total_copy(0).start()
-    each(1, lambda j: near_copy(j, j).wait_send())
-    outside(lambda q, j: far_copy(q, j, me).wait_send())
+    batch(near.at[pl.ds(0, m - 1)], near_send, near_recv).wait_send()
+    batch(far.at[pl.ds(0, n - m)], far_send, far_recv).wait_send()
+    batch(slabs.at[pl.ds(0, planes - 1), :, 0], half_send, half_recv.at[0, 0]).wait_send()
     for part in range(parts):
         own_slab(part, lambda copy: copy.wait_send())
         for step in range(1, planes):
-            q = nearest(step)
-            passed_slab(part, q, lambda copy: copy.wait_send())
-            half_copy(part, q, rep).wait_send()
-        for q in range(planes):
-            each(1, lambda j: pooled_copy(part, q, j, j).wait_send())
-    others(lambda peer: grad_copy(0, peer, me).wait_send())
+            passed_slab(part, nearest(step), lambda copy: copy.wait_send())
+        sent = pooled_out.at[part, :, pl.ds(0, m - 1)]
+        batch(sent, pooled_send.at[part], pooled_recv.at[part]).wait_send()
+
+    def grads_sent(part):
+        sent = grad_out.at[part, pl.ds(0, n - 1)]
+        batch(sent, grad_send.at[part], grad_recv.at[part, 0]).wait_send()
+
+    grads_sent(0)
     dither_copy.wait()
     collect(1)
     total_copy(1).start()
-    others(lambda peer: grad_copy(1, peer, me).wait_send())
+    grads_sent(1)
     for part in range(parts):
         total_copy(part).wait_recv()
 
@@ -501,17 +521,17 @@
             pltpu.VMEM((slab_size, 128), jnp.float32),
             dma((6,)),
             dma((2, PARTS)),
-            dma((m,)),
-            dma((m,)),
-            dma((n,)),
-            dma((n,)),
+            dma(()),
+            dma(()),
+            dma(()),
+            dma(()),
             dma((2, PARTS, planes)),
             dma((PARTS, planes)),
+            dma(()),
             dma((PARTS, planes)),
-            dma((PARTS, planes)),
-            dma((PARTS, planes, m)),
-            dma((PARTS, n)),
-            dma((PARTS, n)),
+            dma((PARTS,)),
+            dma((PARTS,)),
+            dma((PARTS,)),
             dma((PARTS, n)),
         ],
         compiler_params=pltpu.CompilerParams(collective_id=0, has_side_effects=True),

time: 56.6 us -> 55.3 us (0.977)
  Pallas kernels: 55.8 us -> 54 us
    pallas_call x1, Pallas kernels: 54 us -> 52.3 us  [fused_step(): pl.pallas_call(functools.partial(step_kernel, n), out_shape=(pltpu.VMEM((...]
where the time goes in v2:
time: 55.3 us; the launch traced here: 54.7 us
  Pallas kernels  54 us (98%)
  between operations  0.66 us (1%)
    pallas_call x1, Pallas kernels, fused_step(): pl.pallas_call(functools.partial(step_kernel, n), out_shape=(pltpu.VMEM((...  52.3 us
    pallas_call x1, Pallas kernels, write_table(): pl.pallas_call(write_kernel, out_shape=(jax.ShapeDtypeStruct(table.shape,...  1.74 us

profile of v2, /device:TPU:11, one launch (start us, length us, event | category | flops | bytes accessed | tf_op | source)
XLA Modules:
  0.0 54.7 jit_solution(12794988314787682880)
XLA Ops:
  0.6 0.0 copy-start
  0.6 52.3 %fused_step.1 = (bf16[640,256]{1,0:T(8,128)(2,1)S(1)}, f32[24,128]{1,0:T(8,128)S(1)}, bf16[48,64,256]{2,1,0:T(8,128)(2,1)S(1)}) custom-call(s32[2,4,4,4,64]{4,3,2,1,0:T(4,128)} %bitcast.17, s32[2,4,4,4,64]{4,3,2,1,0:T(4,128)} %bitcast.18, bf16[2,16,16,64]{3,2,1,0:T(8,128)(2,1)} %bitcast.16, s32[1,10]{1,0:T(1,128)} %touched_ref.3, f32[24,128]{1,0:T(8,128)} %bitcast.19, ...), custom_call_target="tpu_custom_call" | custom-call | tf_op jit(solution)/shard_map/fused_step/pallas_call | solution.py:492
  52.9 0.0 copy-done
  52.9 1.7 %write_table.1 = (bf16[48,64,256]{2,1,0:T(8,128)(2,1)}, f32[24,128]{1,0:T(8,128)}) custom-call(s32[1,10]{1,0:T(1,128)S(1)} %copy-done, bf16[10,64,256]{2,1,0:T(8,128)(2,1)S(1)} %bitcast.13, f32[24,128]{1,0:T(8,128)S(1)} %get-tuple-element.8.state_ref, bf16[48,64,256]{2,1,0:T(8,128)(2,1)S(1)} %get-tuple-element.9.table_ref), custom_call_target="tpu_custom_call" | custom-call | tf_op jit(solution)/shard_map/write_table/pallas_call | solution.py:577
Async XLA Ops:
  0.6 52.3 %copy-start = (s32[1,10]{1,0:T(1,128)S(1)}, s32[1,10]{1,0:T(1,128)}, u32[]{:S(2)}) copy-start(s32[1,10]{1,0:T(1,128)} %touched_ref.3) | copy-start | bytes 124

commit v3 on v2

--- a/solution.py
+++ b/solution.py
@@ -210,11 +210,6 @@
     each(1, lambda j: near_copy(j, local).start())
     own_slab(0, lambda copy: copy.start())
     outside(lambda q, j: far_copy(q, j, me).start())
-
-    @pl.when(outer)
-    def _():
-        own_slab(1, lambda copy: copy.start())
-
     cot_size = cot_in.shape[1]
 
     def spread(chunk, carry):
@@ -242,6 +237,7 @@
         return carry
 
     lax.fori_loop(0, n, fold, 0)
+    own_slab(1, lambda copy: copy.start())
     total[...] = jnp.zeros_like(total)
 
     offset_in_block = lax.broadcasted_iota(jnp.int32, (BLOCK, samples), 0)
@@ -379,24 +375,22 @@
     @pl.when(inner)
     def _():
         relay(0, 2)
-        own_slab(1, lambda copy: copy.start())
         pool(1, plane)
-        pool_from(0, 1)
-        pool_from(0, 2)
-        relay(0, 3)
         relay(1, 1)
         relay(1, 2)
+        pool_from(0, 1)
+        relay(0, 3)
+        pool_from(0, 2)
         pool_from(0, 3)
+        relay(1, 3)
         pool_from(1, 1)
         pool_from(1, 2)
-        relay(1, 3)
-        pool_from(1, 3)
 
     @pl.when(outer)
     def _():
         pool(1, plane)
+        relay(1, 1)
         pool_from(0, 1)
-        relay(1, 1)
         relay(0, 2)
         pool_from(1, 1)
         pool_from(0, 2)
@@ -405,8 +399,8 @@
         pool_from(1, 2)
         pool_from(0, 3)
         relay(1, 3)
-        pool_from(1, 3)
-
+
+    pool_from(1, 3)
     arrive(0)
     interact(0)
     arrive(1)

time: 55.3 us -> 52.4 us (0.948)
  Pallas kernels: 54 us -> 51.5 us
    pallas_call x1, Pallas kernels: 52.3 us -> 49.8 us  [fused_step(): pl.pallas_call(functools.partial(step_kernel, n), out_shape=(pltpu.VMEM((...]
where the time goes in v3:
time: 52.4 us; the launch traced here: 52.2 us
  Pallas kernels  51.5 us (98%)
  between operations  0.66 us (1%)
    pallas_call x1, Pallas kernels, fused_step(): pl.pallas_call(functools.partial(step_kernel, n), out_shape=(pltpu.VMEM((...  49.8 us
    pallas_call x1, Pallas kernels, write_table(): pl.pallas_call(write_kernel, out_shape=(jax.ShapeDtypeStruct(table.shape,...  1.74 us

profile of v3, /device:TPU:11, one launch (start us, length us, event | category | flops | bytes accessed | tf_op | source)
XLA Modules:
  0.0 52.2 jit_solution(14729234573005791003)
XLA Ops:
  0.6 0.0 copy-start
  0.6 49.8 %fused_step.1 = (bf16[640,256]{1,0:T(8,128)(2,1)S(1)}, f32[24,128]{1,0:T(8,128)S(1)}, bf16[48,64,256]{2,1,0:T(8,128)(2,1)S(1)}) custom-call(s32[2,4,4,4,64]{4,3,2,1,0:T(4,128)} %bitcast.17, s32[2,4,4,4,64]{4,3,2,1,0:T(4,128)} %bitcast.18, bf16[2,16,16,64]{3,2,1,0:T(8,128)(2,1)} %bitcast.16, s32[1,10]{1,0:T(1,128)} %touched_ref.3, f32[24,128]{1,0:T(8,128)} %bitcast.19, ...), custom_call_target="tpu_custom_call" | custom-call | tf_op jit(solution)/shard_map/fused_step/pallas_call | solution.py:486
  50.4 0.0 copy-done
  50.4 1.7 %write_table.1 = (bf16[48,64,256]{2,1,0:T(8,128)(2,1)}, f32[24,128]{1,0:T(8,128)}) custom-call(s32[1,10]{1,0:T(1,128)S(1)} %copy-done, bf16[10,64,256]{2,1,0:T(8,128)(2,1)S(1)} %bitcast.13, f32[24,128]{1,0:T(8,128)S(1)} %get-tuple-element.8.state_ref, bf16[48,64,256]{2,1,0:T(8,128)(2,1)S(1)} %get-tuple-element.9.table_ref), custom_call_target="tpu_custom_call" | custom-call | tf_op jit(solution)/shard_map/write_table/pallas_call | solution.py:571
Async XLA Ops:
  0.6 49.8 %copy-start = (s32[1,10]{1,0:T(1,128)S(1)}, s32[1,10]{1,0:T(1,128)}, u32[]{:S(2)}) copy-start(s32[1,10]{1,0:T(1,128)} %touched_ref.3) | copy-start | bytes 124

commit v4 on v3

--- a/solution.py
+++ b/solution.py
@@ -240,23 +240,34 @@
     own_slab(1, lambda copy: copy.start())
     total[...] = jnp.zeros_like(total)
 
-    offset_in_block = lax.broadcasted_iota(jnp.int32, (BLOCK, samples), 0)
-    offset_in_block = offset_in_block.astype(jnp.float32).astype(jnp.bfloat16)
-    one = jnp.ones((BLOCK, samples), jnp.bfloat16)
+    sublanes = 16
+    place_of = lax.broadcasted_iota(jnp.int32, (BLOCK, samples), 0)
+    place_of = place_of.astype(jnp.float32).astype(jnp.bfloat16)
+    one = jnp.ones((sublanes, samples), jnp.bfloat16)
+    none = jnp.zeros_like(one)
 
     def hits(micros):
         rows = jnp.concatenate([micros[i] for i in range(micros.shape[0])], axis=-1)
-        blocks = []
-        block_of, offset_of = rows // BLOCK, lax.rem(rows, BLOCK)
+        block_of = (rows // BLOCK).astype(jnp.float32)
+        offset_of = lax.rem(rows, BLOCK).astype(jnp.float32)
+
+        def wide(values, lookup):
+            row = jnp.broadcast_to(values[lookup : lookup + 1, :], (sublanes, samples))
+            return row.astype(jnp.bfloat16)
+
+        spans = [slice(at, at + sublanes) for at in range(0, BLOCK, sublanes)]
+        offsets = [wide(offset_of, lookup) for lookup in range(bags)]
+        same = [[jnp.where(offset == place_of[span], one, none) for span in spans] for offset in offsets]
+        in_block = [wide(block_of, lookup) for lookup in range(bags)]
+        pieces = []
         for block in range(slab_size // BLOCK):
-            wanted = jnp.where(block_of == block, offset_of, -1).astype(jnp.float32)
-            counted = jnp.zeros((BLOCK, samples), jnp.bfloat16)
-            for lookup in range(bags):
-                row = jnp.broadcast_to(wanted[lookup : lookup + 1, :], (BLOCK, samples))
-                same = row.astype(jnp.bfloat16) == offset_in_block
-                counted = counted + jnp.where(same, one, jnp.zeros_like(one))
-            blocks.append(counted)
-        return jnp.concatenate(blocks, axis=0)
+            chosen = [row == jnp.full_like(row, block) for row in in_block]
+            for at in range(len(spans)):
+                terms = [jnp.where(chosen[k], same[k][at], none) for k in range(bags)]
+                while len(terms) > 1:
+                    terms = [sum(terms[k + 1 : k + 2], terms[k]) for k in range(0, len(terms), 2)]
+                pieces.append(terms[0])
+        return jnp.concatenate(pieces, axis=0)
 
     def pooled_copy(part, q, j, slot):
         return pltpu.make_async_remote_copy(
@@ -276,25 +287,42 @@
             **at(peer),
         )
 
+    def member(at):
+        return lax.rem(local + at, m)
+
+    def pairs(body):
+        def run(pair, carry):
+            body(pair)
+            return carry
+
+        lax.fori_loop(0, m // 2, run, 0)
+
+    def near_pair(q, pair):
+        return [hits(near[member(2 * pair + k), :, q]) for k in (1, 2)]
+
     def pool(part, q):
         rows_of = slabs[q, part].reshape(columns, slab_size)
 
-        def pooled(j):
+        def both(pair):
             if keeps and part > 0:
-                counted = kept[q, j]
+                counted = kept[q, pair]
             else:
-                counted = hits(near[j, :, q])
+                counted = jnp.concatenate(near_pair(q, pair), axis=1)
                 if keeps:
-                    kept[q, j] = counted
+                    kept[q, pair] = counted
             summed = jnp.dot(rows_of, counted, preferred_element_type=jnp.float32)
-            return summed.astype(jnp.bfloat16)
-
-        def send(j):
-            pooled_out[part, q, j] = pooled(j)
-            pooled_copy(part, q, j, local).start()
-
-        each(1, send)
-        pooled_in[part, q * m + local] = pooled(local)
+            summed = summed.astype(jnp.bfloat16)
+            first, second = member(2 * pair + 1), member(2 * pair + 2)
+            pooled_out[part, q, first] = summed[:, :samples]
+            pooled_copy(part, q, first, local).start()
+            pooled_out[part, q, second] = summed[:, samples:]
+
+            @pl.when(2 * pair + 2 < m)
+            def _():
+                pooled_copy(part, q, second, local).start()
+
+        pairs(both)
+        pooled_in[part, q * m + local] = pooled_out[part, q, local]
 
     def relay(part, step):
         q = nearest(step)
@@ -314,7 +342,7 @@
         arrived = pooled_in.at[part, pl.ds(0, planes * (m - 1))]
         batch(arrived, pooled_send.at[part], pooled_recv.at[part]).wait_recv()
 
-    def interact(part):
+    def interact(part, first=True, rest=True):
         def mixed(feature):
             def add(other, carry):
                 weight = w_ref[pl.ds(feature * n + other, 1), :]
@@ -328,45 +356,56 @@
             grad_copy(part, peer, me).start()
 
         for step in range(planes - 1, 0, -1):
-            q = nearest(step)
-            each(0, lambda j: send(q * m + j))
-        each(1, lambda j: send(plane * m + j))
-        grad_in[part, me] = mixed(me)
-
-    def keep_far(first, last):
-        def take(q, j):
-            peer = q * m + j
-            kept_own[peer] = hits(far[peer])
-
-        if keeps:
-            outside(take, first, last)
-
-    def collect(part):
-        def add(peer, counted):
-            total[part] += lax.dot_general(
-                counted,
-                grad_in[part, peer],
-                (((1,), (1,)), ((), ())),
-                preferred_element_type=jnp.float32,
-            )
-
-        def near_hits(j):
-            return kept[plane, j] if keeps else hits(near[j, :, plane])
-
-        def take_near(j):
-            grad_copy(part, plane * m + j, plane * m + j).wait_recv()
-            add(plane * m + j, near_hits(j))
-
-        def take_far(q, j):
-            peer = q * m + j
-            grad_copy(part, peer, peer).wait_recv()
-            add(peer, kept_own[peer] if keeps else hits(far[peer]))
-
-        add(me, near_hits(local))
-        each(1, take_near)
+            if first if step > 1 else rest:
+                q = nearest(step)
+                each(0, lambda j: send(q * m + j))
+        if rest:
+            each(1, lambda j: send(plane * m + j))
+            grad_in[part, me] = mixed(me)
+
+    def far_pair(q, pair):
+        counted = [hits(far[q * m + member(2 * pair + k)]) for k in (0, 1)]
+        return jnp.concatenate(counted, axis=1)
+
+    def keep_far():
         for step in range(1, planes):
             q = nearest(step)
-            each(0, lambda j: take_far(q, j))
+
+            def take(pair):
+                kept_own[q, pair] = far_pair(q, pair)
+
+            if keeps:
+                pairs(take)
+
+    def collect(part):
+        def add(first, second, counted):
+            grads = jnp.concatenate([grad_in[part, first], grad_in[part, second]], axis=1)
+            total[part] += lax.dot_general(
+                counted, grads, (((1,), (1,)), ((), ())), preferred_element_type=jnp.float32
+            )
+
+        def ready(peer):
+            grad_copy(part, peer, peer).wait_recv()
+
+        def take_near(pair):
+            first, second = (plane * m + member(2 * pair + k) for k in (1, 2))
+            ready(first)
+            pl.when(2 * pair + 2 < m)(lambda: ready(second))
+            if keeps:
+                add(first, second, kept[plane, pair])
+            else:
+                add(first, second, jnp.concatenate(near_pair(plane, pair), axis=1))
+
+        def take_far(q, pair):
+            first, second = (q * m + member(2 * pair + k) for k in (0, 1))
+            ready(first)
+            ready(second)
+            add(first, second, kept_own[q, pair] if keeps else far_pair(q, pair))
+
+        pairs(take_near)
+        for step in range(1, planes):
+            q = nearest(step)
+            pairs(lambda pair: take_far(q, pair))
 
     batch(near.at[pl.ds(0, m - 1)], near_send, near_recv).wait_recv()
     pool(0, plane)
@@ -376,21 +415,25 @@
     def _():
         relay(0, 2)
         pool(1, plane)
+        pool_from(0, 1)
         relay(1, 1)
         relay(1, 2)
-        pool_from(0, 1)
+        pool_from(0, 2)
         relay(0, 3)
-        pool_from(0, 2)
+        pool_from(1, 1)
         pool_from(0, 3)
         relay(1, 3)
-        pool_from(1, 1)
         pool_from(1, 2)
+        arrive(0)
+        interact(0, rest=False)
+        pool_from(1, 3)
+        interact(0, first=False)
 
     @pl.when(outer)
     def _():
         pool(1, plane)
+        pool_from(0, 1)
         relay(1, 1)
-        pool_from(0, 1)
         relay(0, 2)
         pool_from(1, 1)
         pool_from(0, 2)
@@ -399,14 +442,14 @@
         pool_from(1, 2)
         pool_from(0, 3)
         relay(1, 3)
-
-    pool_from(1, 3)
-    arrive(0)
-    interact(0)
+        pool_from(1, 3)
+        arrive(0)
+        interact(0)
+
     arrive(1)
     interact(1)
     batch(far.at[pl.ds(0, n - m)], far_send, far_recv).wait_recv()
-    keep_far(0, n - m)
+    keep_far()
     state_copy.wait()
     pieces = []
     for block in range(touch_count):
@@ -478,6 +521,7 @@
     slab_size, width = dither.shape
     columns = width // PARTS
     keeps = 2 * n * slab_size * samples <= KEEP_BYTES
+    held = (planes, m // 2) if keeps else (1, 1)
     dma = pltpu.SemaphoreType.DMA
     block = (PARTS, n, columns, samples)
     vmem = pl.BlockSpec(memory_space=pltpu.VMEM)
@@ -508,8 +552,8 @@
             pltpu.VMEM(block, jnp.bfloat16),
             pltpu.VMEM(block, jnp.bfloat16),
             pltpu.VMEM(block, jnp.bfloat16),
-            pltpu.VMEM((planes if keeps else 1, m if keeps else 1, slab_size, samples), jnp.bfloat16),
-            pltpu.VMEM((n if keeps else 1, slab_size, samples), jnp.bfloat16),
+            pltpu.VMEM(held + (slab_size, 2 * samples), jnp.bfloat16),
+            pltpu.VMEM(held + (slab_size, 2 * samples), jnp.bfloat16),
             pltpu.VMEM((PARTS, slab_size, columns), jnp.float32),
             pltpu.VMEM((PARTS, slab_size, columns), jnp.float32),
             pltpu.VMEM((slab_size, 128), jnp.float32),

time: 52.4 us -> 51.7 us (0.987)
  Pallas kernels: 51.5 us -> 50.9 us
    pallas_call x1, Pallas kernels: 49.8 us -> 49.1 us  [fused_step(): pl.pallas_call(functools.partial(step_kernel, n), out_shape=(pltpu.VMEM((...]
where the time goes in v4:
time: 51.7 us; the launch traced here: 51.5 us
  Pallas kernels  50.9 us (98%)
  between operations  0.66 us (1%)
    pallas_call x1, Pallas kernels, fused_step(): pl.pallas_call(functools.partial(step_kernel, n), out_shape=(pltpu.VMEM((...  49.1 us
    pallas_call x1, Pallas kernels, write_table(): pl.pallas_call(write_kernel, out_shape=(jax.ShapeDtypeStruct(table.shape,...  1.74 us

profile of v4, /device:TPU:11, one launch (start us, length us, event | category | flops | bytes accessed | tf_op | source)
XLA Modules:
  0.0 51.5 jit_solution(1355481243998757786)
XLA Ops:
  0.6 0.0 copy-start
  0.6 49.1 %fused_step.1 = (bf16[640,256]{1,0:T(8,128)(2,1)S(1)}, f32[24,128]{1,0:T(8,128)S(1)}, bf16[48,64,256]{2,1,0:T(8,128)(2,1)S(1)}) custom-call(s32[2,4,4,4,64]{4,3,2,1,0:T(4,128)} %bitcast.17, s32[2,4,4,4,64]{4,3,2,1,0:T(4,128)} %bitcast.18, bf16[2,16,16,64]{3,2,1,0:T(8,128)(2,1)} %bitcast.16, s32[1,10]{1,0:T(1,128)} %touched_ref.3, f32[24,128]{1,0:T(8,128)} %bitcast.19, ...), custom_call_target="tpu_custom_call" | custom-call | tf_op jit(solution)/shard_map/fused_step/pallas_call | solution.py:530
  49.8 0.0 copy-done
  49.8 1.7 %write_table.1 = (bf16[48,64,256]{2,1,0:T(8,128)(2,1)}, f32[24,128]{1,0:T(8,128)}) custom-call(s32[1,10]{1,0:T(1,128)S(1)} %copy-done, bf16[10,64,256]{2,1,0:T(8,128)(2,1)S(1)} %bitcast.13, f32[24,128]{1,0:T(8,128)S(1)} %get-tuple-element.8.state_ref, bf16[48,64,256]{2,1,0:T(8,128)(2,1)S(1)} %get-tuple-element.9.table_ref), custom_call_target="tpu_custom_call" | custom-call | tf_op jit(solution)/shard_map/write_table/pallas_call | solution.py:615
Async XLA Ops:
  0.6 49.2 %copy-start = (s32[1,10]{1,0:T(1,128)S(1)}, s32[1,10]{1,0:T(1,128)}, u32[]{:S(2)}) copy-start(s32[1,10]{1,0:T(1,128)} %touched_ref.3) | copy-start | bytes 124

commit v5 on v4

--- a/solution.py
+++ b/solution.py
@@ -10,7 +10,10 @@
 
 BLOCK = 64
 PLANES = 4
-PARTS = 2
+UNITS = 4
+UNROLL = 4
+PARTS = ((0, 1), (1, 1), (2, 2))
+HALVES = ((0, 2, (0, 1)), (2, 2, (2,)))
 LEARN_RATE = 0.1
 POOL_DECAY = 0.5
 DITHER_UNIT = 2.0 ** (-15)
@@ -80,17 +83,18 @@
     pooled_recv,
     grad_send,
     grad_recv,
+    grad_last,
 ):
     me = lax.axis_index("mp")
     rep = lax.axis_index("rep")
-    planes, parts = slabs.shape[0], slabs.shape[1]
+    planes, parts = slabs.shape[0], len(PARTS)
     m = n // planes
     plane = me // m
     local = lax.rem(me, m)
     samples = w_ref.shape[1]
     bags = rows_ref.shape[3]
     slab_size, width = slab.shape
-    columns = width // parts
+    columns = width // UNITS
     touch_count = slab_size // BLOCK
     keeps = kept.shape[0] == planes
 
@@ -122,6 +126,13 @@
 
     def nearest(step):
         return plane_order(planes, plane, step)
+
+    def units(part):
+        first, count = PARTS[part]
+        return pl.ds(first, count)
+
+    def tall(part):
+        return PARTS[part][1] * columns
 
     barrier = pltpu.get_barrier_semaphore()
     others(lambda peer: pl.semaphore_signal(barrier, inc=1, **at(peer)))
@@ -143,9 +154,8 @@
     table_copy.wait()
     for block in range(touch_count):
         slab[block * BLOCK : (block + 1) * BLOCK, :] = table_in[touched_ref[0, block]]
-    for part in range(parts):
-        turned = slab[:, part * columns : (part + 1) * columns].astype(jnp.float32).T
-        slabs[plane, part] = turned.astype(jnp.bfloat16).reshape(slabs.shape[2:])
+    turned = slab[...].astype(jnp.float32).T.astype(jnp.bfloat16)
+    slabs[plane] = turned.reshape(slabs.shape[1:])
     pl.semaphore_wait(barrier, n)
 
     def near_copy(j, slot):
@@ -166,19 +176,19 @@
             **at(q * m + j),
         )
 
-    def slab_copy(part, q, way, peer):
+    def slab_copy(part, q, slot, peer):
         return pltpu.make_async_remote_copy(
-            slabs.at[q, part, rep],
-            slabs.at[q, part, rep],
-            slab_send.at[way, part, q],
+            slabs.at[q, units(part), rep],
+            slabs.at[q, units(part), rep],
+            slab_send.at[part, slot],
             slab_recv.at[part, q],
             **at(peer),
         )
 
     def half_copy(part, q, which):
         return pltpu.make_async_remote_copy(
-            slabs.at[q, part, which],
-            slabs.at[q, part, which],
+            slabs.at[q, units(part), which],
+            slabs.at[q, units(part), which],
             half_send,
             half_recv.at[part, q],
             **partner,
@@ -192,20 +202,20 @@
     def own_slab(part, act):
         @pl.when(has_up)
         def _():
-            act(slab_copy(part, plane, 0, up))
+            act(slab_copy(part, plane, plane, up))
 
         @pl.when(has_down)
         def _():
-            act(slab_copy(part, plane, 1, down))
+            act(slab_copy(part, plane, planes, down))
 
     def passed_slab(part, q, act):
         @pl.when(jnp.logical_and(q < plane, has_up))
         def _():
-            act(slab_copy(part, q, 0, up))
+            act(slab_copy(part, q, q, up))
 
         @pl.when(jnp.logical_and(q > plane, has_down))
         def _():
-            act(slab_copy(part, q, 1, down))
+            act(slab_copy(part, q, q, down))
 
     each(1, lambda j: near_copy(j, local).start())
     own_slab(0, lambda copy: copy.start())
@@ -237,7 +247,8 @@
         return carry
 
     lax.fori_loop(0, n, fold, 0)
-    own_slab(1, lambda copy: copy.start())
+    for part in range(1, parts):
+        own_slab(part, lambda copy: copy.start())
     total[...] = jnp.zeros_like(total)
 
     sublanes = 16
@@ -271,8 +282,8 @@
 
     def pooled_copy(part, q, j, slot):
         return pltpu.make_async_remote_copy(
-            pooled_out.at[part, q, j],
-            pooled_in.at[part, q * m + slot],
+            pooled_out.at[units(part), q, j],
+            pooled_in.at[units(part), q * m + slot],
             pooled_send.at[part],
             pooled_recv.at[part],
             **at(plane * m + j),
@@ -280,10 +291,10 @@
 
     def grad_copy(part, peer, slot):
         return pltpu.make_async_remote_copy(
-            grad_out.at[part, peer],
-            grad_in.at[part, slot],
+            grad_out.at[units(part), peer],
+            grad_in.at[units(part), slot],
             grad_send.at[part],
-            grad_recv.at[part, slot],
+            grad_last.at[slot] if part == parts - 1 else grad_recv.at[part, slot // m],
             **at(peer),
         )
 
@@ -301,7 +312,7 @@
         return [hits(near[member(2 * pair + k), :, q]) for k in (1, 2)]
 
     def pool(part, q):
-        rows_of = slabs[q, part].reshape(columns, slab_size)
+        rows_of = slabs[q, units(part)].reshape(tall(part), slab_size)
 
         def both(pair):
             if keeps and part > 0:
@@ -311,22 +322,22 @@
                 if keeps:
                     kept[q, pair] = counted
             summed = jnp.dot(rows_of, counted, preferred_element_type=jnp.float32)
-            summed = summed.astype(jnp.bfloat16)
+            summed = summed.astype(jnp.bfloat16).reshape(-1, columns, 2 * samples)
             first, second = member(2 * pair + 1), member(2 * pair + 2)
-            pooled_out[part, q, first] = summed[:, :samples]
+            pooled_out[units(part), q, first] = summed[:, :, :samples]
             pooled_copy(part, q, first, local).start()
-            pooled_out[part, q, second] = summed[:, samples:]
+            pooled_out[units(part), q, second] = summed[:, :, samples:]
 
             @pl.when(2 * pair + 2 < m)
             def _():
                 pooled_copy(part, q, second, local).start()
 
         pairs(both)
-        pooled_in[part, q * m + local] = pooled_out[part, q, local]
+        pooled_in[units(part), q * m + local] = pooled_out[units(part), q, local]
 
     def relay(part, step):
         q = nearest(step)
-        slab_copy(part, q, 0, up).wait_recv()
+        slab_copy(part, q, q, up).wait_recv()
         passed_slab(part, q, lambda copy: copy.start())
         half_copy(part, q, rep).start()
 
@@ -339,20 +350,22 @@
         return pltpu.make_async_remote_copy(ref, ref, send_sem, recv_sem, **partner)
 
     def arrive(part):
-        arrived = pooled_in.at[part, pl.ds(0, planes * (m - 1))]
+        arrived = pooled_in.at[units(part), pl.ds(0, planes * (m - 1))]
         batch(arrived, pooled_send.at[part], pooled_recv.at[part]).wait_recv()
 
     def interact(part, first=True, rest=True):
         def mixed(feature):
             def add(other, carry):
                 weight = w_ref[pl.ds(feature * n + other, 1), :]
-                return carry + weight * pooled_in[part, other].astype(jnp.float32)
-
-            start = jnp.zeros((columns, samples), jnp.float32)
-            return lax.fori_loop(0, n, add, start, unroll=4).astype(jnp.bfloat16)
+                seen = pooled_in[units(part), other].reshape(tall(part), samples)
+                return carry + weight * seen.astype(jnp.float32)
+
+            start = jnp.zeros((tall(part), samples), jnp.float32)
+            mix = lax.fori_loop(0, n, add, start, unroll=UNROLL)
+            return mix.astype(jnp.bfloat16).reshape(-1, columns, samples)
 
         def send(peer):
-            grad_out[part, peer] = mixed(peer)
+            grad_out[units(part), peer] = mixed(peer)
             grad_copy(part, peer, me).start()
 
         for step in range(planes - 1, 0, -1):
@@ -361,7 +374,7 @@
                 each(0, lambda j: send(q * m + j))
         if rest:
             each(1, lambda j: send(plane * m + j))
-            grad_in[part, me] = mixed(me)
+            grad_in[units(part), me] = mixed(me)
 
     def far_pair(q, pair):
         counted = [hits(far[q * m + member(2 * pair + k)]) for k in (0, 1)]
@@ -377,15 +390,28 @@
             if keeps:
                 pairs(take)
 
-    def collect(part):
+    def collect(which):
+        first_unit, count, members = HALVES[which]
+
         def add(first, second, counted):
-            grads = jnp.concatenate([grad_in[part, first], grad_in[part, second]], axis=1)
-            total[part] += lax.dot_general(
-                counted, grads, (((1,), (1,)), ((), ())), preferred_element_type=jnp.float32
+            grads = [grad_in[pl.ds(first_unit, count), peer] for peer in (first, second)]
+            grads = [piece.reshape(count * columns, samples) for piece in grads]
+            total[which] += lax.dot_general(
+                counted,
+                jnp.concatenate(grads, axis=1),
+                (((1,), (1,)), ((), ())),
+                preferred_element_type=jnp.float32,
             )
 
+        def plane_ready(q, blocks):
+            for part in members:
+                if part < parts - 1:
+                    arrived = grad_in.at[units(part), pl.ds(0, blocks)]
+                    batch(arrived, grad_send.at[part], grad_recv.at[part, q]).wait_recv()
+
         def ready(peer):
-            grad_copy(part, peer, peer).wait_recv()
+            if parts - 1 in members:
+                grad_copy(parts - 1, peer, peer).wait_recv()
 
         def take_near(pair):
             first, second = (plane * m + member(2 * pair + k) for k in (1, 2))
@@ -402,9 +428,11 @@
             ready(second)
             add(first, second, kept_own[q, pair] if keeps else far_pair(q, pair))
 
+        plane_ready(plane, m - 1)
         pairs(take_near)
         for step in range(1, planes):
-            q = nearest(step)
+            q = jnp.where(inner, nearest(step % (planes - 1) + 1), nearest(step))
+            plane_ready(q, m)
             pairs(lambda pair: take_far(q, pair))
 
     batch(near.at[pl.ds(0, m - 1)], near_send, near_recv).wait_recv()
@@ -415,39 +443,56 @@
     def _():
         relay(0, 2)
         pool(1, plane)
-        pool_from(0, 1)
         relay(1, 1)
         relay(1, 2)
+        pool_from(0, 1)
         pool_from(0, 2)
         relay(0, 3)
+        relay(2, 1)
+        relay(2, 2)
         pool_from(1, 1)
+        relay(1, 3)
         pool_from(0, 3)
-        relay(1, 3)
         pool_from(1, 2)
+        pool_from(1, 3)
+        pool(2, plane)
+        relay(2, 3)
         arrive(0)
-        interact(0, rest=False)
-        pool_from(1, 3)
-        interact(0, first=False)
+        interact(0)
+        pool_from(2, 1)
+        arrive(1)
+        interact(1)
+        pool_from(2, 2)
+        pool_from(2, 3)
 
     @pl.when(outer)
     def _():
         pool(1, plane)
+        relay(1, 1)
         pool_from(0, 1)
-        relay(1, 1)
+        relay(2, 1)
+        pool_from(1, 1)
         relay(0, 2)
-        pool_from(1, 1)
+        relay(1, 2)
         pool_from(0, 2)
-        relay(1, 2)
+        pool_from(1, 2)
+        pool(2, plane)
         relay(0, 3)
-        pool_from(1, 2)
+        relay(2, 2)
+        relay(1, 3)
         pool_from(0, 3)
-        relay(1, 3)
         pool_from(1, 3)
+        pool_from(2, 1)
+        pool_from(2, 2)
         arrive(0)
         interact(0)
-
-    arrive(1)
-    interact(1)
+        relay(2, 3)
+        pool_from(2, 3)
+        arrive(1)
+        interact(1)
+
+    arrive(2)
+    interact(2)
     batch(far.at[pl.ds(0, n - m)], far_send, far_recv).wait_recv()
     keep_far()
     state_copy.wait()
@@ -472,24 +517,25 @@
         own_slab(part, lambda copy: copy.wait_send())
         for step in range(1, planes):
             passed_slab(part, nearest(step), lambda copy: copy.wait_send())
-        sent = pooled_out.at[part, :, pl.ds(0, m - 1)]
+        sent = pooled_out.at[units(part), :, pl.ds(0, m - 1)]
         batch(sent, pooled_send.at[part], pooled_recv.at[part]).wait_send()
 
     def grads_sent(part):
-        sent = grad_out.at[part, pl.ds(0, n - 1)]
-        batch(sent, grad_send.at[part], grad_recv.at[part, 0]).wait_send()
+        sent = grad_out.at[units(part), pl.ds(0, n - 1)]
+        batch(sent, grad_send.at[part], grad_last.at[0]).wait_send()
 
     grads_sent(0)
+    grads_sent(1)
     dither_copy.wait()
     collect(1)
     total_copy(1).start()
-    grads_sent(1)
-    for part in range(parts):
-        total_copy(part).wait_recv()
+    grads_sent(2)
+    for which in range(len(HALVES)):
+        total_copy(which).wait_recv()
 
     def update(block, carry):
         at_rows = pl.ds(pl.multiple_of(block * BLOCK, BLOCK), BLOCK)
-        grad = [total[part, at_rows, :] + total_in[part, at_rows, :] for part in range(parts)]
+        grad = [total[h, at_rows, :] + total_in[h, at_rows, :] for h in range(len(HALVES))]
         grad = jnp.concatenate(grad, axis=1)
         state_next = state_col[at_rows, :] + jnp.sum(grad * grad, axis=1, keepdims=True) / width
         state_col[at_rows, :] = state_next
@@ -509,8 +555,8 @@
         piece = jnp.broadcast_to(jnp.concatenate([piece, piece], axis=1), state_all.shape)
         state_all = jnp.where(block_at == touched_ref[0, block], piece, state_all)
     state_out_ref[...] = state_all
-    for part in range(parts):
-        total_copy(part).wait_send()
+    for which in range(len(HALVES)):
+        total_copy(which).wait_send()
 
 
 def fused_step(n, blocks, offsets, cot, touched, state, table, dither):
@@ -519,11 +565,11 @@
     samples = micros * sample_count
     cot_size = math.gcd(n, 16)
     slab_size, width = dither.shape
-    columns = width // PARTS
+    columns, parts = width // UNITS, len(PARTS)
     keeps = 2 * n * slab_size * samples <= KEEP_BYTES
     held = (planes, m // 2) if keeps else (1, 1)
     dma = pltpu.SemaphoreType.DMA
-    block = (PARTS, n, columns, samples)
+    block = (UNITS, n, columns, samples)
     vmem = pl.BlockSpec(memory_space=pltpu.VMEM)
     smem = pl.BlockSpec(memory_space=pltpu.SMEM)
     hbm = pl.BlockSpec(memory_space=pltpu.HBM)
@@ -547,30 +593,31 @@
             pltpu.VMEM((n * n, samples), jnp.float32),
             pltpu.VMEM((slab_size, width), jnp.int32),
             pltpu.VMEM((slab_size, width), jnp.bfloat16),
-            pltpu.VMEM((planes, PARTS, 2, columns // 2, slab_size), jnp.bfloat16),
-            pltpu.VMEM((PARTS, planes, m, columns, samples), jnp.bfloat16),
+            pltpu.VMEM((planes, UNITS, 2, columns // 2, slab_size), jnp.bfloat16),
+            pltpu.VMEM((UNITS, planes, m, columns, samples), jnp.bfloat16),
             pltpu.VMEM(block, jnp.bfloat16),
             pltpu.VMEM(block, jnp.bfloat16),
             pltpu.VMEM(block, jnp.bfloat16),
             pltpu.VMEM(held + (slab_size, 2 * samples), jnp.bfloat16),
             pltpu.VMEM(held + (slab_size, 2 * samples), jnp.bfloat16),
-            pltpu.VMEM((PARTS, slab_size, columns), jnp.float32),
-            pltpu.VMEM((PARTS, slab_size, columns), jnp.float32),
+            pltpu.VMEM((len(HALVES), slab_size, width // len(HALVES)), jnp.float32),
+            pltpu.VMEM((len(HALVES), slab_size, width // len(HALVES)), jnp.float32),
             pltpu.VMEM((slab_size, 128), jnp.float32),
             dma((6,)),
-            dma((2, PARTS)),
+            dma((2, len(HALVES))),
             dma(()),
             dma(()),
             dma(()),
             dma(()),
-            dma((2, PARTS, planes)),
-            dma((PARTS, planes)),
+            dma((parts, planes + 1)),
+            dma((parts, planes)),
             dma(()),
-            dma((PARTS, planes)),
-            dma((PARTS,)),
-            dma((PARTS,)),
-            dma((PARTS,)),
-            dma((PARTS, n)),
+            dma((parts, planes)),
+            dma((parts,)),
+            dma((parts,)),
+            dma((parts,)),
+            dma((parts - 1, planes)),
+            dma((n,)),
         ],
         compiler_params=pltpu.CompilerParams(collective_id=0, has_side_effects=True),
         name="fused_step",

time: 51.7 us -> 49.5 us (0.957)
  Pallas kernels: 50.9 us -> 48.6 us
    pallas_call x1, Pallas kernels: 49.1 us -> 46.9 us  [fused_step(): pl.pallas_call(functools.partial(step_kernel, n), out_shape=(pltpu.VMEM((...]
where the time goes in v5:
time: 49.5 us; the launch traced here: 49.3 us
  Pallas kernels  48.6 us (98%)
  between operations  0.66 us (1%)
    pallas_call x1, Pallas kernels, fused_step(): pl.pallas_call(functools.partial(step_kernel, n), out_shape=(pltpu.VMEM((...  46.9 us
    pallas_call x1, Pallas kernels, write_table(): pl.pallas_call(write_kernel, out_shape=(jax.ShapeDtypeStruct(table.shape,...  1.74 us

profile of v5, /device:TPU:11, one launch (start us, length us, event | category | flops | bytes accessed | tf_op | source)
XLA Modules:
  0.0 49.3 jit_solution(3012969427589004433)
XLA Ops:
  0.6 0.0 copy-start
  0.6 46.9 %fused_step.1 = (bf16[640,256]{1,0:T(8,128)(2,1)S(1)}, f32[24,128]{1,0:T(8,128)S(1)}, bf16[48,64,256]{2,1,0:T(8,128)(2,1)S(1)}) custom-call(s32[2,4,4,4,64]{4,3,2,1,0:T(4,128)} %bitcast.17, s32[2,4,4,4,64]{4,3,2,1,0:T(4,128)} %bitcast.18, bf16[2,16,16,64]{3,2,1,0:T(8,128)(2,1)} %bitcast.16, s32[1,10]{1,0:T(1,128)} %touched_ref.3, f32[24,128]{1,0:T(8,128)} %bitcast.19, ...), custom_call_target="tpu_custom_call" | custom-call | tf_op jit(solution)/shard_map/fused_step/pallas_call | solution.py:576
  47.5 0.0 copy-done
  47.5 1.7 %write_table.1 = (bf16[48,64,256]{2,1,0:T(8,128)(2,1)}, f32[24,128]{1,0:T(8,128)}) custom-call(s32[1,10]{1,0:T(1,128)S(1)} %copy-done, bf16[10,64,256]{2,1,0:T(8,128)(2,1)S(1)} %bitcast.13, f32[24,128]{1,0:T(8,128)S(1)} %get-tuple-element.8.state_ref, bf16[48,64,256]{2,1,0:T(8,128)(2,1)S(1)} %get-tuple-element.9.table_ref), custom_call_target="tpu_custom_call" | custom-call | tf_op jit(solution)/shard_map/write_table/pallas_call | solution.py:662
Async XLA Ops:
  0.6 46.9 %copy-start = (s32[1,10]{1,0:T(1,128)S(1)}, s32[1,10]{1,0:T(1,128)}, u32[]{:S(2)}) copy-start(s32[1,10]{1,0:T(1,128)} %touched_ref.3) | copy-start | bytes 124

commit v6 on v5

--- a/solution.py
+++ b/solution.py
@@ -12,6 +12,7 @@
 PLANES = 4
 UNITS = 4
 UNROLL = 4
+CHUNKS = 2
 PARTS = ((0, 1), (1, 1), (2, 2))
 HALVES = ((0, 2, (0, 1)), (2, 2, (2,)))
 LEARN_RATE = 0.1
@@ -24,8 +25,9 @@
 
 def dither_round(weights, dither_bits):
     magnitude = jnp.maximum(jnp.abs(weights), SMALLEST)
-    spacing = jnp.exp2(jnp.floor(jnp.log2(magnitude)) - 7.0)
-    grid_level = jnp.floor(weights / spacing + dither_bits.astype(jnp.float32) * DITHER_UNIT)
+    exponent = jnp.floor(jnp.log2(magnitude)) - 7.0
+    spacing, per_spacing = jnp.exp2(exponent), jnp.exp2(-exponent)
+    grid_level = jnp.floor(weights * per_spacing + dither_bits.astype(jnp.float32) * DITHER_UNIT)
     return (grid_level * spacing).astype(jnp.bfloat16)
 
 
@@ -46,7 +48,6 @@
     state_hbm,
     table_ref,
     dither_ref,
-    out_ref,
     state_out_ref,
     table_in,
     block_ref,
@@ -62,6 +63,7 @@
     slabs,
     pooled_out,
     pooled_in,
+    wide,
     grad_out,
     grad_in,
     kept,
@@ -137,7 +139,9 @@
     barrier = pltpu.get_barrier_semaphore()
     others(lambda peer: pl.semaphore_signal(barrier, inc=1, **at(peer)))
     pl.semaphore_signal(barrier, inc=1, **partner)
-    table_copy = pltpu.make_async_copy(table_ref, table_in, local_sem.at[0])
+    table_blocks = table_ref.shape[0]
+    held_table = table_in.at[pl.ds(0, table_blocks)]
+    table_copy = pltpu.make_async_copy(table_ref, held_table, local_sem.at[0])
     table_copy.start()
     block_copy = pltpu.make_async_copy(block_hbm, block_ref, local_sem.at[1])
     block_copy.start()
@@ -180,7 +184,7 @@
         return pltpu.make_async_remote_copy(
             slabs.at[q, units(part), rep],
             slabs.at[q, units(part), rep],
-            slab_send.at[part, slot],
+            slab_send.at[slot],
             slab_recv.at[part, q],
             **at(peer),
         )
@@ -202,20 +206,20 @@
     def own_slab(part, act):
         @pl.when(has_up)
         def _():
-            act(slab_copy(part, plane, plane, up))
+            act(slab_copy(part, plane, 0, up))
 
         @pl.when(has_down)
         def _():
-            act(slab_copy(part, plane, planes, down))
+            act(slab_copy(part, plane, 0, down))
 
     def passed_slab(part, q, act):
         @pl.when(jnp.logical_and(q < plane, has_up))
         def _():
-            act(slab_copy(part, q, q, up))
+            act(slab_copy(part, q, 1, up))
 
         @pl.when(jnp.logical_and(q > plane, has_down))
         def _():
-            act(slab_copy(part, q, q, down))
+            act(slab_copy(part, q, 1, down))
 
     each(1, lambda j: near_copy(j, local).start())
     own_slab(0, lambda copy: copy.start())
@@ -337,7 +341,7 @@
 
     def relay(part, step):
         q = nearest(step)
-        slab_copy(part, q, q, up).wait_recv()
+        slab_copy(part, q, 1, up).wait_recv()
         passed_slab(part, q, lambda copy: copy.start())
         half_copy(part, q, rep).start()
 
@@ -352,11 +356,24 @@
     def arrive(part):
         arrived = pooled_in.at[units(part), pl.ds(0, planes * (m - 1))]
         batch(arrived, pooled_send.at[part], pooled_recv.at[part]).wait_recv()
+        widen(part)
+
+    def widen(part):
+        if wide.shape[0] == n:
+
+            def run(other, carry):
+                seen = pooled_in[units(part), other].reshape(tall(part), samples)
+                wide[other, : tall(part)] = seen.astype(jnp.float32)
+                return carry
+
+            lax.fori_loop(0, n, run, 0, unroll=4)
 
     def interact(part, first=True, rest=True):
         def mixed(feature):
             def add(other, carry):
                 weight = w_ref[pl.ds(feature * n + other, 1), :]
+                if wide.shape[0] == n:
+                    return carry + weight * wide[other, : tall(part)]
                 seen = pooled_in[units(part), other].reshape(tall(part), samples)
                 return carry + weight * seen.astype(jnp.float32)
 
@@ -503,20 +520,36 @@
         pieces.append(jnp.where(lax.rem(at_block, 2) == 0, pair[:, :BLOCK], pair[:, BLOCK:]))
     state_row = jnp.concatenate(pieces, axis=1)
     state_col[...] = jnp.broadcast_to(state_row, (state_col.shape[1], slab_size)).T
-    def total_copy(part):
+    chunk = touch_count // CHUNKS * BLOCK
+
+    def total_copy(which, at):
+        span = pl.ds(at * chunk, chunk)
         return pltpu.make_async_remote_copy(
-            total.at[part], total_in.at[part], pair_sem.at[0, part], pair_sem.at[1, part], **partner
+            total.at[which, span],
+            total_in.at[which, span],
+            pair_sem.at[0, which, at],
+            pair_sem.at[1, which, at],
+            **partner,
         )
 
     collect(0)
-    total_copy(0).start()
+    for at_chunk in range(CHUNKS):
+        total_copy(0, at_chunk).start()
     batch(near.at[pl.ds(0, m - 1)], near_send, near_recv).wait_send()
     batch(far.at[pl.ds(0, n - m)], far_send, far_recv).wait_send()
     batch(slabs.at[pl.ds(0, planes - 1), :, 0], half_send, half_recv.at[0, 0]).wait_send()
+    any_slab = slab_recv.at[0, 0]
+
+    @pl.when(inner)
+    def _():
+        batch(slabs.at[pl.ds(0, 2), :, 0], slab_send.at[0], any_slab).wait_send()
+        batch(slabs.at[pl.ds(0, planes - 1), :, 0], slab_send.at[1], any_slab).wait_send()
+
+    @pl.when(outer)
+    def _():
+        batch(slabs.at[0, :, 0], slab_send.at[0], any_slab).wait_send()
+
     for part in range(parts):
-        own_slab(part, lambda copy: copy.wait_send())
-        for step in range(1, planes):
-            passed_slab(part, nearest(step), lambda copy: copy.wait_send())
         sent = pooled_out.at[units(part), :, pl.ds(0, m - 1)]
         batch(sent, pooled_send.at[part], pooled_recv.at[part]).wait_send()
 
@@ -528,24 +561,26 @@
     grads_sent(1)
     dither_copy.wait()
     collect(1)
-    total_copy(1).start()
+    for at_chunk in range(CHUNKS):
+        total_copy(1, at_chunk).start()
     grads_sent(2)
-    for which in range(len(HALVES)):
-        total_copy(which).wait_recv()
-
     def update(block, carry):
         at_rows = pl.ds(pl.multiple_of(block * BLOCK, BLOCK), BLOCK)
         grad = [total[h, at_rows, :] + total_in[h, at_rows, :] for h in range(len(HALVES))]
         grad = jnp.concatenate(grad, axis=1)
         state_next = state_col[at_rows, :] + jnp.sum(grad * grad, axis=1, keepdims=True) / width
         state_col[at_rows, :] = state_next
-        divisor = jnp.sqrt(state_next) + 1e-08
-        divisor = jnp.concatenate([divisor] * (width // divisor.shape[1]), axis=1)
-        moved = slab[at_rows, :].astype(jnp.float32) - LEARN_RATE * grad / divisor
-        out_ref[at_rows, :] = dither_round(moved, dither_in[at_rows, :])
+        rate = LEARN_RATE / (jnp.sqrt(state_next) + 1e-08)
+        rate = jnp.concatenate([rate] * (width // rate.shape[1]), axis=1)
+        moved = slab[at_rows, :].astype(jnp.float32) - grad * rate
+        table_in[table_blocks + block] = dither_round(moved, dither_in[at_rows, :])
         return carry
 
-    lax.fori_loop(0, touch_count, update, 0, unroll=2)
+    per_chunk = touch_count // CHUNKS
+    for at_chunk in range(CHUNKS):
+        for which in range(len(HALVES)):
+            total_copy(which, at_chunk).wait_recv()
+        lax.fori_loop(at_chunk * per_chunk, (at_chunk + 1) * per_chunk, update, 0, unroll=True)
     state_all = state_ref[...]
     block_at = 2 * lax.broadcasted_iota(jnp.int32, state_all.shape, 0)
     block_at = block_at + lax.broadcasted_iota(jnp.int32, state_all.shape, 1) // BLOCK
@@ -556,7 +591,8 @@
         state_all = jnp.where(block_at == touched_ref[0, block], piece, state_all)
     state_out_ref[...] = state_all
     for which in range(len(HALVES)):
-        total_copy(which).wait_send()
+        for at_chunk in range(CHUNKS):
+            total_copy(which, at_chunk).wait_send()
 
 
 def fused_step(n, blocks, offsets, cot, touched, state, table, dither):
@@ -576,12 +612,11 @@
     return pl.pallas_call(
         functools.partial(step_kernel, n),
         out_shape=(
-            pltpu.VMEM((slab_size, width), jnp.bfloat16),
             pltpu.VMEM(state.shape, jnp.float32),
-            pltpu.VMEM(table.shape, jnp.bfloat16),
+            pltpu.VMEM((table.shape[0] + slab_size // BLOCK,) + table.shape[1:], jnp.bfloat16),
         ),
         in_specs=[hbm, hbm, hbm, smem, hbm, hbm, hbm],
-        out_specs=(vmem, vmem, vmem),
+        out_specs=(vmem, vmem),
         scratch_shapes=[
             pltpu.VMEM(blocks.shape, jnp.int32),
             pltpu.VMEM(blocks.shape, jnp.int32),
@@ -596,6 +631,7 @@
             pltpu.VMEM((planes, UNITS, 2, columns // 2, slab_size), jnp.bfloat16),
             pltpu.VMEM((UNITS, planes, m, columns, samples), jnp.bfloat16),
             pltpu.VMEM(block, jnp.bfloat16),
+            pltpu.VMEM((n if keeps else 1, 2 * columns, samples), jnp.float32),
             pltpu.VMEM(block, jnp.bfloat16),
             pltpu.VMEM(block, jnp.bfloat16),
             pltpu.VMEM(held + (slab_size, 2 * samples), jnp.bfloat16),
@@ -604,12 +640,12 @@
             pltpu.VMEM((len(HALVES), slab_size, width // len(HALVES)), jnp.float32),
             pltpu.VMEM((slab_size, 128), jnp.float32),
             dma((6,)),
-            dma((2, len(HALVES))),
+            dma((2, len(HALVES), CHUNKS)),
             dma(()),
             dma(()),
             dma(()),
             dma(()),
-            dma((parts, planes + 1)),
+            dma((2,)),
             dma((parts, planes)),
             dma(()),
             dma((parts, planes)),
@@ -624,48 +660,32 @@
     )(blocks, offsets, cot, touched, state, table, dither)
 
 
-def write_kernel(touched_ref, new_ref, state_ref, table_ref, out_ref, state_out_ref, place, sem):
+def write_kernel(touched_ref, state_ref, blocks_ref, out_ref, state_out_ref, place, sem):
     state_copy = pltpu.make_async_copy(state_ref, state_out_ref, sem.at[1])
     state_copy.start()
-    blocks, touch_count = table_ref.shape[0], touched_ref.shape[1]
-
-    def clear(block, carry):
-        place[block] = -1
-        return carry
-
-    lax.fori_loop(0, blocks, clear, 0, unroll=8)
+    blocks, touch_count = out_ref.shape[0], touched_ref.shape[1]
+    for block in range(blocks):
+        place[block] = block
     for i in range(touch_count):
-        place[touched_ref[0, i]] = i
-
-    def write(block, carry):
-        new = place[block]
-
-        @pl.when(new >= 0)
-        def _():
-            pltpu.make_async_copy(new_ref.at[new], out_ref.at[block], sem.at[0]).start()
-
-        @pl.when(new < 0)
-        def _():
-            pltpu.make_async_copy(table_ref.at[block], out_ref.at[block], sem.at[0]).start()
-
-        return carry
-
-    lax.fori_loop(0, blocks, write, 0)
-    pltpu.make_async_copy(table_ref, out_ref, sem.at[0]).wait()
+        place[touched_ref[0, i]] = blocks + i
+    for block in range(blocks):
+        source = blocks_ref.at[place[block]]
+        pltpu.make_async_copy(source, out_ref.at[block], sem.at[0]).start()
+    pltpu.make_async_copy(blocks_ref.at[pl.ds(0, blocks)], out_ref, sem.at[0]).wait()
     state_copy.wait()
 
 
-def write_table(touched, new_rows, state, table):
+def write_table(touched, state, blocks, table):
     vmem = pl.BlockSpec(memory_space=pltpu.VMEM)
     hbm = pl.BlockSpec(memory_space=pltpu.HBM)
-    held = [pltpu.with_memory_space_constraint(x, pltpu.VMEM) for x in (new_rows, state, table)]
+    held = [pltpu.with_memory_space_constraint(x, pltpu.VMEM) for x in (state, blocks)]
     return pl.pallas_call(
         write_kernel,
         out_shape=(
             jax.ShapeDtypeStruct(table.shape, table.dtype),
             jax.ShapeDtypeStruct(state.shape, state.dtype),
         ),
-        in_specs=[pl.BlockSpec(memory_space=pltpu.SMEM), vmem, vmem, vmem],
+        in_specs=[pl.BlockSpec(memory_space=pltpu.SMEM), vmem, vmem],
         out_specs=(hbm, hbm),
         scratch_shapes=[pltpu.SMEM((table.shape[0],), jnp.int32), pltpu.SemaphoreType.DMA((2,))],
         compiler_params=pltpu.CompilerParams(vmem_limit_bytes=4 << 20),
@@ -679,18 +699,16 @@
     micro_count, sample_count, feature_count, bag_count = lookup_block.shape
     n = lax.axis_size("mp")
     row_count, emb_width = table.shape
-    touch_count = touched_blocks.shape[1]
     split = (micro_count, PLANES, feature_count // PLANES, bag_count, sample_count)
     blocks = lookup_block.transpose(0, 2, 3, 1).reshape(split)
     offsets = lookup_offset.transpose(0, 2, 3, 1).reshape(split)
     cot = interaction_grad.transpose(0, 2, 3, 1)
     table_blocks = table.reshape(row_count // BLOCK, BLOCK, emb_width)
     state = adagrad_state.reshape(row_count // (2 * BLOCK), 2 * BLOCK)
-    new_rows, new_state, table_copy = fused_step(
+    new_state, held_blocks = fused_step(
         n, blocks, offsets, cot, touched_blocks, state, table_blocks, dither[0]
     )
-    new_rows = new_rows.reshape(touch_count, BLOCK, emb_width)
-    new_table, new_state = write_table(touched_blocks, new_rows, new_state, table_copy)
+    new_table, new_state = write_table(touched_blocks, new_state, held_blocks, table_blocks)
     return (new_table.reshape(row_count, emb_width), new_state.reshape(row_count))
 
 

time: 49.5 us -> 48.8 us (0.986)
  Pallas kernels: 48.6 us -> 47.9 us
    pallas_call x1, Pallas kernels: 46.9 us -> 46.2 us  [fused_step(): pl.pallas_call(functools.partial(step_kernel, n), out_shape=(pltpu.VMEM(s...]
where the time goes in v6:
time: 48.8 us; the launch traced here: 48.6 us
  Pallas kernels  47.9 us (98%)
  between operations  0.66 us (1%)
    pallas_call x1, Pallas kernels, fused_step(): pl.pallas_call(functools.partial(step_kernel, n), out_shape=(pltpu.VMEM(s...  46.2 us
    pallas_call x1, Pallas kernels, write_table(): pl.pallas_call(write_kernel, out_shape=(jax.ShapeDtypeStruct(table.shape,...  1.71 us

profile of v6, /device:TPU:11, one launch (start us, length us, event | category | flops | bytes accessed | tf_op | source)
XLA Modules:
  0.0 48.6 jit_solution(2267784325873696322)
XLA Ops:
  0.6 0.0 copy-start
  0.6 46.2 %fused_step.1 = (f32[24,128]{1,0:T(8,128)S(1)}, bf16[58,64,256]{2,1,0:T(8,128)(2,1)S(1)}) custom-call(s32[2,4,4,4,64]{4,3,2,1,0:T(4,128)} %bitcast.15, s32[2,4,4,4,64]{4,3,2,1,0:T(4,128)} %bitcast.16, bf16[2,16,16,64]{3,2,1,0:T(8,128)(2,1)} %bitcast.14, s32[1,10]{1,0:T(1,128)} %touched_ref.3, f32[24,128]{1,0:T(8,128)} %bitcast.17, ...), custom_call_target="tpu_custom_call" | custom-call | tf_op jit(solution)/shard_map/fused_step/pallas_call | solution.py:612
  46.9 0.0 copy-done
  46.9 1.7 %write_table.1 = (bf16[48,64,256]{2,1,0:T(8,128)(2,1)}, f32[24,128]{1,0:T(8,128)}) custom-call(s32[1,10]{1,0:T(1,128)S(1)} %copy-done, f32[24,128]{1,0:T(8,128)S(1)} %get-tuple-element.6.state_ref, bf16[58,64,256]{2,1,0:T(8,128)(2,1)S(1)} %get-tuple-element.7.blocks_ref), custom_call_target="tpu_custom_call" | custom-call | tf_op jit(solution)/shard_map/write_table/pallas_call | solution.py:682
Async XLA Ops:
  0.6 46.3 %copy-start = (s32[1,10]{1,0:T(1,128)S(1)}, s32[1,10]{1,0:T(1,128)}, u32[]{:S(2)}) copy-start(s32[1,10]{1,0:T(1,128)} %touched_ref.3) | copy-start | bytes 124

commit v7 on v6

--- a/solution.py
+++ b/solution.py
@@ -358,12 +358,16 @@
         batch(arrived, pooled_send.at[part], pooled_recv.at[part]).wait_recv()
         widen(part)
 
+    def wide_rows(part):
+        start = PARTS[part][0] * columns % wide.shape[1]
+        return slice(start, start + tall(part))
+
     def widen(part):
         if wide.shape[0] == n:
 
             def run(other, carry):
                 seen = pooled_in[units(part), other].reshape(tall(part), samples)
-                wide[other, : tall(part)] = seen.astype(jnp.float32)
+                wide[other, wide_rows(part)] = seen.astype(jnp.float32)
                 return carry
 
             lax.fori_loop(0, n, run, 0, unroll=4)
@@ -373,7 +377,7 @@
             def add(other, carry):
                 weight = w_ref[pl.ds(feature * n + other, 1), :]
                 if wide.shape[0] == n:
-                    return carry + weight * wide[other, : tall(part)]
+                    return carry + weight * wide[other, wide_rows(part)]
                 seen = pooled_in[units(part), other].reshape(tall(part), samples)
                 return carry + weight * seen.astype(jnp.float32)
 
@@ -502,11 +506,13 @@
         pool_from(2, 1)
         pool_from(2, 2)
         arrive(0)
-        interact(0)
+        interact(0, rest=False)
         relay(2, 3)
         pool_from(2, 3)
         arrive(1)
-        interact(1)
+        interact(1, rest=False)
+        interact(0, first=False)
+        interact(1, first=False)
 
     arrive(2)
     interact(2)

time: 48.8 us -> 48.7 us (level)
    pallas_call x1, Pallas kernels: 46.2 us -> 45.7 us  [fused_step(): pl.pallas_call(functools.partial(step_kernel, n), out_shape=(pltpu.VMEM(s...]
where the time goes in v7:
time: 48.7 us; the launch traced here: 48.1 us
  Pallas kernels  47.5 us (98%)
  between operations  0.66 us (1%)
    pallas_call x1, Pallas kernels, fused_step(): pl.pallas_call(functools.partial(step_kernel, n), out_shape=(pltpu.VMEM(s...  45.7 us
    pallas_call x1, Pallas kernels, write_table(): pl.pallas_call(write_kernel, out_shape=(jax.ShapeDtypeStruct(table.shape,...  1.71 us

profile of v7, /device:TPU:11, one launch (start us, length us, event | category | flops | bytes accessed | tf_op | source)
XLA Modules:
  0.0 48.1 jit_solution(13037402527018389611)
XLA Ops:
  0.6 0.0 copy-start
  0.6 45.7 %fused_step.1 = (f32[24,128]{1,0:T(8,128)S(1)}, bf16[58,64,256]{2,1,0:T(8,128)(2,1)S(1)}) custom-call(s32[2,4,4,4,64]{4,3,2,1,0:T(4,128)} %bitcast.15, s32[2,4,4,4,64]{4,3,2,1,0:T(4,128)} %bitcast.16, bf16[2,16,16,64]{3,2,1,0:T(8,128)(2,1)} %bitcast.14, s32[1,10]{1,0:T(1,128)} %touched_ref.3, f32[24,128]{1,0:T(8,128)} %bitcast.17, ...), custom_call_target="tpu_custom_call" | custom-call | tf_op jit(solution)/shard_map/fused_step/pallas_call | solution.py:618
  46.4 0.0 copy-done
  46.4 1.7 %write_table.1 = (bf16[48,64,256]{2,1,0:T(8,128)(2,1)}, f32[24,128]{1,0:T(8,128)}) custom-call(s32[1,10]{1,0:T(1,128)S(1)} %copy-done, f32[24,128]{1,0:T(8,128)S(1)} %get-tuple-element.6.state_ref, bf16[58,64,256]{2,1,0:T(8,128)(2,1)S(1)} %get-tuple-element.7.blocks_ref), custom_call_target="tpu_custom_call" | custom-call | tf_op jit(solution)/shard_map/write_table/pallas_call | solution.py:688
Async XLA Ops:
  0.6 45.8 %copy-start = (s32[1,10]{1,0:T(1,128)S(1)}, s32[1,10]{1,0:T(1,128)}, u32[]{:S(2)}) copy-start(s32[1,10]{1,0:T(1,128)} %touched_ref.3) | copy-start | bytes 124

commit v8 on v7

--- a/solution.py
+++ b/solution.py
@@ -11,7 +11,7 @@
 BLOCK = 64
 PLANES = 4
 UNITS = 4
-UNROLL = 4
+UNROLL = 16
 CHUNKS = 2
 PARTS = ((0, 1), (1, 1), (2, 2))
 HALVES = ((0, 2, (0, 1)), (2, 2, (2,)))
@@ -391,7 +391,7 @@
 
         for step in range(planes - 1, 0, -1):
             if first if step > 1 else rest:
-                q = nearest(step)
+                q = jnp.where(outer, nearest(step if step < 2 else planes + 1 - step), nearest(step))
                 each(0, lambda j: send(q * m + j))
         if rest:
             each(1, lambda j: send(plane * m + j))

time: 48.7 us -> 48.7 us (level)
  no operation moved by 1% of the time
where the time goes in v8:
time: 48.7 us; the launch traced here: 48.2 us
  Pallas kernels  47.5 us (98%)
  between operations  0.66 us (1%)
    pallas_call x1, Pallas kernels, fused_step(): pl.pallas_call(functools.partial(step_kernel, n), out_shape=(pltpu.VMEM(s...  45.8 us
    pallas_call x1, Pallas kernels, write_table(): pl.pallas_call(write_kernel, out_shape=(jax.ShapeDtypeStruct(table.shape,...  1.71 us

profile of v8, /device:TPU:11, one launch (start us, length us, event | category | flops | bytes accessed | tf_op | source)
XLA Modules:
  0.0 48.2 jit_solution(11447627667575892417)
XLA Ops:
  0.6 0.0 copy-start
  0.6 45.8 %fused_step.1 = (f32[24,128]{1,0:T(8,128)S(1)}, bf16[58,64,256]{2,1,0:T(8,128)(2,1)S(1)}) custom-call(s32[2,4,4,4,64]{4,3,2,1,0:T(4,128)} %bitcast.15, s32[2,4,4,4,64]{4,3,2,1,0:T(4,128)} %bitcast.16, bf16[2,16,16,64]{3,2,1,0:T(8,128)(2,1)} %bitcast.14, s32[1,10]{1,0:T(1,128)} %touched_ref.3, f32[24,128]{1,0:T(8,128)} %bitcast.17, ...), custom_call_target="tpu_custom_call" | custom-call | tf_op jit(solution)/shard_map/fused_step/pallas_call | solution.py:618
  46.5 0.0 copy-done
  46.5 1.7 %write_table.1 = (bf16[48,64,256]{2,1,0:T(8,128)(2,1)}, f32[24,128]{1,0:T(8,128)}) custom-call(s32[1,10]{1,0:T(1,128)S(1)} %copy-done, f32[24,128]{1,0:T(8,128)S(1)} %get-tuple-element.6.state_ref, bf16[58,64,256]{2,1,0:T(8,128)(2,1)S(1)} %get-tuple-element.7.blocks_ref), custom_call_target="tpu_custom_call" | custom-call | tf_op jit(solution)/shard_map/write_table/pallas_call | solution.py:688
Async XLA Ops:
  0.6 45.8 %copy-start = (s32[1,10]{1,0:T(1,128)S(1)}, s32[1,10]{1,0:T(1,128)}, u32[]{:S(2)}) copy-start(s32[1,10]{1,0:T(1,128)} %touched_ref.3) | copy-start | bytes 124
